TPU v7x, 512 devices: a whole 4x8x8 slice. The times are simulated.
512 devices in a mesh: cell: 512 (over x, z, y, core).
Axes of the slice: x: 4, y: 8, z: 8, core: 2. Of those that a mesh axis runs over, the one named last changes fastest.
Arguments:
- features: bfloat16 [131072, 512], P('cell'), may hold values from -6 to 6
- radial: bfloat16 [131072, 8, 128], P('cell'), may hold values from 0 to 1
- neighbours: int32 [131072, 8], P('cell'), may hold values from 0 to 131071, as said below
- counts: int32 [131072], P('cell'), may hold values from 1 to 8, as said below
- cotangent: bfloat16 [131072, 8, 256], P('cell'), may hold values from -6 to 6
- w_self: bfloat16 [512, 512], replicated, may hold values from -0.25 to 0.25
- w_neighbour: bfloat16 [512, 512], replicated, may hold values from -0.25 to 0.25
- w_radial: bfloat16 [128, 512], replicated, may hold values from -0.5 to 0.5
- w_block: bfloat16 [512, 256], replicated, may hold values from -0.25 to 0.25
Outputs:
- blocks: bfloat16 [131072, 8, 256], P('cell')
- feat_grad: bfloat16 [131072, 512], P('cell')
Inputs may be any that keep to these rules, and one draw needn't show every extreme that they name: `neighbours`: each neighbour index differs from its atom's index by 1 to 128. Only the first counts[i] slots of atom i are live, the rest are padding.
All inputs are finite; a program needn't handle non-finite values.
Results may differ from a plain program's by a relative error of at most 0.013.
Values may be sent and summed in bfloat16 or wider, within the bound.
A program may use at most 64 MiB of HBM per device.

v0:
```python
import math

import jax
import jax.numpy as jnp
from jax import lax
from jax.sharding import PartitionSpec as P


def extended(block, sides, width):
    for axis, dim in sides:
        count = lax.axis_size(axis)
        forward = [(i, i + 1) for i in range(count - 1)]
        backward = [(target, source) for source, target in forward]
        low = lax.ppermute(
            lax.slice_in_dim(block, block.shape[dim] - width, None, axis=dim), axis, forward
        )
        high = lax.ppermute(lax.slice_in_dim(block, 0, width, axis=dim), axis, backward)
        block = jnp.concatenate([low, block, high], axis=dim)
    return block


def shifted(value, axis, steps):
    count = lax.axis_size(axis)
    initial, last = (max(0, -steps), min(count, count - steps))
    return lax.ppermute(value, axis, [(source, source + steps) for source in range(initial, last)])


def window_pick(table, rows, atoms_per, slot_count, step, width):
    block_total = rows.shape[0] // (atoms_per * slot_count)
    grouped = rows.reshape(block_total, atoms_per * slot_count)
    columns = jnp.arange(width, dtype=jnp.int32)

    def one_block(packed):
        index, ids = packed
        start = index * step
        window = lax.dynamic_slice_in_dim(table, start, width, 0)
        picker = ((ids - start)[:, None] == columns[None, :]).astype(jnp.bfloat16)
        return jnp.dot(picker, window, preferred_element_type=jnp.float32).astype(jnp.bfloat16)

    picked = lax.map(one_block, (jnp.arange(block_total, dtype=jnp.int32), grouped))
    return picked.reshape(-1, table.shape[1])


def window_add(values, rows, total_rows, atoms_per, slot_count, step, width):
    feat_width = values.shape[1]
    block_total = rows.shape[0] // (atoms_per * slot_count)
    grouped = rows.reshape(block_total, atoms_per * slot_count)
    grouped_vals = values.reshape(block_total, atoms_per * slot_count, feat_width)
    columns = jnp.arange(width, dtype=jnp.int32)
    contract = (((0,), (0,)), ((), ()))

    def one_block(carry, packed):
        index, ids, block_vals = packed
        start = index * step
        picker = ((ids - start)[:, None] == columns[None, :]).astype(jnp.bfloat16)
        high = block_vals.astype(jnp.bfloat16)
        low = (block_vals - high.astype(jnp.float32)).astype(jnp.bfloat16)
        added = lax.dot_general(picker, high, contract, preferred_element_type=jnp.float32)
        added = added + lax.dot_general(picker, low, contract, preferred_element_type=jnp.float32)
        window = lax.dynamic_slice_in_dim(carry, start, width, 0)
        carry = lax.dynamic_update_slice_in_dim(carry, window + added, start, 0)
        return (carry, None)

    start_sum = jnp.zeros((total_rows, feat_width), jnp.float32)
    summed, unused = lax.scan(
        one_block, start_sum, (jnp.arange(block_total, dtype=jnp.int32), grouped, grouped_vals)
    )
    return summed


def body(features, radial, neighbours, counts, cotangent, w_self, w_neighbour, w_radial, w_block):
    atoms_here = features.shape[0]
    feat_width = features.shape[1]
    slot_count = neighbours.shape[1]
    block_width = w_block.shape[1]
    radial_width = radial.shape[2]
    margin = atoms_here // 2
    atom_block = math.gcd(atoms_here, 128)
    window_rows = atom_block + 2 * margin
    offset = lax.axis_index("cell") * atoms_here - margin
    local_rows = (neighbours - offset).reshape(-1)
    self_proj = jnp.dot(features, w_self, preferred_element_type=jnp.float32).astype(jnp.bfloat16)
    padded_feat = extended(features, (("cell", 0),), margin)
    padded_proj = jnp.dot(padded_feat, w_neighbour, preferred_element_type=jnp.float32).astype(
        jnp.bfloat16
    )
    gathered = window_pick(padded_proj, local_rows, atom_block, slot_count, atom_block, window_rows)
    gathered = gathered.reshape(atoms_here, slot_count, feat_width)
    radial_flat = radial.reshape(-1, radial_width)
    radial_gate = jnp.dot(radial_flat, w_radial, preferred_element_type=jnp.float32).reshape(
        atoms_here, slot_count, feat_width
    )
    slot_index = jnp.arange(slot_count, dtype=jnp.int32)
    live_mask = (slot_index[None, :] < counts[:, None]).astype(jnp.float32)[:, :, None]
    pre_act = (
        self_proj.astype(jnp.float32)[:, None, :] + gathered.astype(jnp.float32)
    ) * radial_gate
    message = (jax.nn.silu(pre_act) * live_mask).astype(jnp.bfloat16)
    blocks = jnp.dot(
        message.reshape(-1, feat_width), w_block, preferred_element_type=jnp.float32
    ).astype(jnp.bfloat16)
    blocks = blocks.reshape(atoms_here, slot_count, block_width)
    d_message = jnp.dot(
        cotangent.reshape(-1, block_width), w_block.T, preferred_element_type=jnp.float32
    )
    d_message = d_message.reshape(atoms_here, slot_count, feat_width)
    sigmoid_val = jax.nn.sigmoid(pre_act)
    adjoint = (
        d_message * live_mask * (sigmoid_val * (1.0 + pre_act * (1.0 - sigmoid_val))) * radial_gate
    )
    self_adj = jnp.sum(adjoint, axis=1).astype(jnp.bfloat16)
    padded_adj = window_add(
        adjoint.reshape(-1, feat_width),
        local_rows,
        atoms_here + 2 * margin,
        atom_block,
        slot_count,
        atom_block,
        window_rows,
    )
    lower_rim = padded_adj[:margin]
    own_adj = padded_adj[margin : margin + atoms_here]
    upper_rim = padded_adj[margin + atoms_here :]
    from_above = shifted(lower_rim.astype(jnp.bfloat16), "cell", -1).astype(lower_rim.dtype)
    from_below = shifted(upper_rim.astype(jnp.bfloat16), "cell", 1).astype(upper_rim.dtype)
    summed_adj = own_adj + jnp.concatenate([from_below, from_above], axis=0)
    nbr_adj = summed_adj.astype(jnp.bfloat16)
    feat_grad = jnp.dot(self_adj, w_self.T, preferred_element_type=jnp.float32) + jnp.dot(
        nbr_adj, w_neighbour.T, preferred_element_type=jnp.float32
    )
    return (blocks, feat_grad.astype(jnp.bfloat16))


def solution(mesh):
    in_specs = (
        P("cell", None),
        P("cell", None, None),
        P("cell", None),
        P("cell"),
        P("cell", None, None),
        P(),
        P(),
        P(),
        P(),
    )
    out_specs = (P("cell", None, None), P("cell", None))
    return jax.shard_map(body, mesh=mesh, in_specs=in_specs, out_specs=out_specs, check_vma=False)
```

profile of v0, /device:TPU:6, one launch (start us, length us, event | category | flops | bytes accessed | tf_op | source)
XLA Modules:
  0.0 75.8 jit_solution(17427253451797441813)
XLA Ops:
  0.6 1.0 %fusion.49 = (bf16[128,512]{1,0:T(8,128)(2,1)S(1)}, bf16[128,512]{1,0:T(8,128)(2,1)S(1)}) fusion(bf16[256,512]{1,0:T(8,128)(2,1)} %param.13), kind=kLoop, calls=%fused_computation.61 | loop fusion | bytes 524288 | tf_op jit(solution)/shard_map/slice | solution.py:15
  1.7 13.6 %collective-permute-start.1 = (bf16[128,512]{1,0:T(8,128)(2,1)S(1)}, bf16[128,512]{1,0:T(8,128)(2,1)S(1)}, u32[]{:S(2)}, u32[]{:S(2)}) collective-permute-start(bf16[128,512]{1,0:T(8,128)(2,1)S(1)} %get-tuple-element.115), channel_id=1, source_target_pairs={{1,0},{2,1},{3,2},{4,3},{5,4},{6,5},{7,6},{8,7},{9,8},{10,9},{11,1... | collective-permute-start | bytes 393224 | tf_op jit(solution)/shard_map/ppermute | solution.py:17
  15.3 1.9 %collective-permute-start = (bf16[128,512]{1,0:T(8,128)(2,1)S(1)}, bf16[128,512]{1,0:T(8,128)(2,1)}, u32[]{:S(2)}, u32[]{:S(2)}) collective-permute-start(bf16[128,512]{1,0:T(8,128)(2,1)S(1)} %get-tuple-element.114), channel_id=1, source_target_pairs={{0,1},{1,2},{2,3},{3,4},{4,5},{5,6},{6,7},{7,8},{8,9},{9,10},{10,1... | collective-permute-start | bytes 393224 | tf_op jit(solution)/shard_map/ppermute | solution.py:14
  17.2 0.7 broadcast_subtract_fusion
  17.9 0.1 copy.14
  18.2 1.4 %fusion.29 = f32[256,512]{1,0:T(8,128)S(1)} fusion(bf16[256,512]{1,0:T(8,128)(2,1)} %param.13, bf16[512,512]{1,0:T(8,128)(2,1)} %param.18), kind=kOutput, calls=%fused_computation.38 | convolution fusion | flops 134479872 | bytes 1310720 | tf_op jit(solution)/shard_map/dot_general | solution.py:82
  19.6 0.7 fusion.45
  20.3 5.6 %collective-permute-done = bf16[128,512]{1,0:T(8,128)(2,1)} collective-permute-done((bf16[128,512]{1,0:T(8,128)(2,1)S(1)}, bf16[128,512]{1,0:T(8,128)(2,1)}, u32[]{:S(2)}, u32[]{:S(2)}) %collective-permute-start) | collective-permute-done | bytes 131104 | tf_op jit(solution)/shard_map/ppermute | solution.py:14
  25.9 2.2 %convolution_convert_fusion.1 = bf16[512,512]{1,0:T(8,128)(2,1)} fusion(bf16[512,512]{1,0:T(8,128)(2,1)S(1)} %copy-done, bf16[128,512]{1,0:T(8,128)(2,1)S(1)} %collective-permute-done.1, bf16[256,512]{1,0:T(8,128)(2,1)} %param.13, bf16[128,512]{1,0:T(8,128)(2,1)} %collective-permute-done), kind=kOutput, calls=%fused_computation.34 | convolution fusion | flops 270270464 | bytes 1572864 | tf_op jit(solution)/shard_map/dot_general | solution.py:84
  28.1 5.9 %while.22 = (s32[]{:T(128)}, bf16[2,1024,512]{2,1,0:T(8,128)(2,1)S(1)}, s32[2,1024]{1,0:T(2,128)S(1)}, s32[2]{0:T(128)S(1)}, bf16[512,512]{1,0:T(8,128)(2,1)}, /...) while((s32[]{:T(128)}, bf16[2,1024,512]{2,1,0:T(8,128)(2,1)S(1)}, s32[2,1024]{1,0:T(2,128)S(1)}, ...), condition=%wide.region_1.2_spmd.clone, body=%wide.region_0.1_spmd.clone.sunk | while | flops 403571712 | bytes 1454255 | solution.py:40
  28.1 0.6 dynamic_slice.53
  29.3 1.8 %fusion.65 = bf16[2,1024,512]{2,1,0:T(8,128)(2,1)S(1)} fusion(bf16[2,1024,512]{2,1,0:T(8,128)(2,1)S(1)} %get-tuple-element.192, s32[]{:T(128)S(6)} %copy.45, s32[1024]{0:T(1024)S(1)} %bitcast.63, bf16[512,512]{1,0:T(8,128)(2,1)} %get-tuple-element.204, s32[]{:T(128)S(6)} %select_n.11), kind=kOutput, calls=%fused_computation.6.clone.1 | convolution fusion | flops 403570688 | bytes 1445896 | tf_op jit(solution)/shard_map/while/body/eval_jaxpr/dot_general | solution.py:38
  31.1 0.6 dynamic_slice.53
  32.2 1.8 %fusion.65 = bf16[2,1024,512]{2,1,0:T(8,128)(2,1)S(1)} fusion(bf16[2,1024,512]{2,1,0:T(8,128)(2,1)S(1)} %get-tuple-element.192, s32[]{:T(128)S(6)} %copy.45, s32[1024]{0:T(1024)S(1)} %bitcast.63, bf16[512,512]{1,0:T(8,128)(2,1)} %get-tuple-element.204, s32[]{:T(128)S(6)} %select_n.11), kind=kOutput, calls=%fused_computation.6.clone.1 | convolution fusion | flops 403570688 | bytes 1445896 | tf_op jit(solution)/shard_map/while/body/eval_jaxpr/dot_general | solution.py:38
  34.0 0.6 convert.7
  34.6 0.4 copy-done.3
  35.1 3.0 %multiply_convert_fusion = (bf16[256,8,512]{2,0,1:T(8,128)(2,1)S(1)}, f32[256,8,512]{2,0,1:T(8,128)S(1)}) fusion(f32[256,8,512]{2,1,0:T(8,128)S(1)} %convert.7, f32[256,8]{0,1:T(8,128)S(1)} %fusion.45, f32[256,512]{1,0:T(8,128)S(1)} %fusion.29, bf16[128,512]{1,0:T(8,128)(2,1)S(1)} %copy-done.5, bf16[256,8,128]{2,1,0:T(8,128)(2,1)S(1)} %copy-done.3), kind=kOutput, calls=%fused_computation.28 | convolution fusion | flops 276824064 | bytes 11673600 | tf_op jit(solution)/shard_map/dot_general | solution.py:90
  38.1 2.3 %fusion.25 = bf16[256,8,256]{2,1,0:T(8,128)(2,1)} fusion(bf16[512,256]{1,0:T(8,128)(2,1)S(1)} %copy-done.4, bf16[256,8,512]{2,0,1:T(8,128)(2,1)S(1)} %get-tuple-element.116), kind=kOutput, calls=%fused_computation.33 | convolution fusion | flops 537395200 | bytes 3407872 | tf_op jit(solution)/shard_map/dot_general | solution.py:99
  40.4 4.1 %fusion.50 = (bf16[256,512]{1,0:T(8,128)(2,1)S(1)}, f32[256,8,512]{2,0,1:T(8,128)S(1)}) fusion(f32[256,8,512]{2,0,1:T(8,128)S(1)} %get-tuple-element.117, f32[256,8,512]{2,1,0:T(8,128)S(1)} %convert.7, f32[256,512]{1,0:T(8,128)S(1)} %fusion.29, f32[256,8]{0,1:T(8,128)S(1)} %fusion.45, bf16[512,256]{1,0:T(8,128)(2,1)S(1)} %copy-done.4, ...), kind=kOutput, calls=%fused_computation.62 | convolution fusion | flops 550371328 | bytes 14688256 | tf_op jit(solution)/shard_map/dot_general | solution.py:103
  44.5 4.4 %copy.19 = f32[256,8,512]{2,1,0:T(8,128)} copy(f32[256,8,512]{2,0,1:T(8,128)S(1)} %get-tuple-element.119) | data formatting | bytes 8388608 | tf_op jit(solution)/shard_map/mul | solution.py:109
  49.1 12.8 %while.23 = (s32[]{:T(128)}, f32[512,512]{1,0:T(8,128)S(1)}, s32[2]{0:T(128)S(1)}, s32[2,1024]{1,0:T(2,128)S(1)}, f32[2,1024,512]{2,1,0:T(8,128)}, /*index=5*/s32[]{:T(128)}, s32[1]{0:T(128)}, s32[]{:T(128)}, s32[]{:T(128)}) while((s32[]{:T(128)}, f32[512,512]{1,0:T(8,128)S(1)}, s32[2]{0:T(128)S(1)}, s32[2,1024]{1,0:T(2,128)S(1)}, ...), condition=%wide.region_4.5_spmd.clone, body=%wide.region_3.4_spmd.clone.sunk | while | flops 808584192 | bytes 6308019 | solution.py:65
  49.1 0.6 dynamic_slice.58
  50.3 2.5 %fusion.67 = f32[384,512]{1,0:T(8,128)S(1)} fusion(f32[2,1024,512]{2,1,0:T(8,128)} %get-tuple-element.231, s32[]{:T(128)S(6)} %copy.51, s32[1024]{0:T(1024)S(1)} %bitcast.61), kind=kOutput, calls=%fused_computation.15.clone.1 | convolution fusion | flops 405143552 | bytes 2887684 | tf_op jit(solution)/shard_map/while/body/eval_jaxpr/dot_general | solution.py:59
  52.9 2.6 %fusion.68 = f32[512,512]{1,0:T(8,128)S(1)} fusion(f32[512,512]{1,0:T(8,128)S(1)} %get-tuple-element.219, s32[]{:T(128)S(6)} %select_n.12, f32[384,512]{1,0:T(8,128)S(1)} %fusion.67, s32[1024]{0:T(1024)S(1)} %bitcast.62, f32[2,1024,512]{2,1,0:T(8,128)} %get-tuple-element.231, s32[]{:T(128)S(6)} %copy.51), kind=kOutput, calls=%fused_computation.19.clone.1 | convolution fusion | flops 403439616 | bytes 3411976 | tf_op jit(solution)/shard_map/while/body/eval_jaxpr/dot_general | solution.py:58
  55.5 0.6 dynamic_slice.58
  56.7 2.5 %fusion.67 = f32[384,512]{1,0:T(8,128)S(1)} fusion(f32[2,1024,512]{2,1,0:T(8,128)} %get-tuple-element.231, s32[]{:T(128)S(6)} %copy.51, s32[1024]{0:T(1024)S(1)} %bitcast.61), kind=kOutput, calls=%fused_computation.15.clone.1 | convolution fusion | flops 405143552 | bytes 2887684 | tf_op jit(solution)/shard_map/while/body/eval_jaxpr/dot_general | solution.py:59
  59.3 2.6 %fusion.68 = f32[512,512]{1,0:T(8,128)S(1)} fusion(f32[512,512]{1,0:T(8,128)S(1)} %get-tuple-element.219, s32[]{:T(128)S(6)} %select_n.12, f32[384,512]{1,0:T(8,128)S(1)} %fusion.67, s32[1024]{0:T(1024)S(1)} %bitcast.62, f32[2,1024,512]{2,1,0:T(8,128)} %get-tuple-element.231, s32[]{:T(128)S(6)} %copy.51), kind=kOutput, calls=%fused_computation.19.clone.1 | convolution fusion | flops 403439616 | bytes 3411976 | tf_op jit(solution)/shard_map/while/body/eval_jaxpr/dot_general | solution.py:58
  62.0 2.3 %collective-permute-start.3 = (bf16[128,512]{1,0:T(8,128)(2,1)S(1)}, bf16[128,512]{1,0:T(8,128)(2,1)S(1)}, u32[]{:S(2)}, u32[]{:S(2)}) collective-permute-start(bf16[128,512]{1,0:T(8,128)(2,1)S(1)} %get-tuple-element.113), channel_id=1, source_target_pairs={{1,0},{2,1},{3,2},{4,3},{5,4},{6,5},{7,6},{8,7},{9,8},{10,9},{11,1... | collective-permute-start | bytes 393224 | tf_op jit(solution)/shard_map/ppermute | solution.py:25
  64.2 2.1 %collective-permute-start.2 = (bf16[128,512]{1,0:T(8,128)(2,1)S(1)}, bf16[128,512]{1,0:T(8,128)(2,1)S(1)}, u32[]{:S(2)}, u32[]{:S(2)}) collective-permute-start(bf16[128,512]{1,0:T(8,128)(2,1)S(1)} %get-tuple-element.112), channel_id=1, source_target_pairs={{0,1},{1,2},{2,3},{3,4},{4,5},{5,6},{6,7},{7,8},{8,9},{9,10},{10,1... | collective-permute-start | bytes 393224 | tf_op jit(solution)/shard_map/ppermute | solution.py:25
  66.3 0.3 fusion.51
  66.7 8.0 %collective-permute-done.2 = bf16[128,512]{1,0:T(8,128)(2,1)S(1)} collective-permute-done((bf16[128,512]{1,0:T(8,128)(2,1)S(1)}, bf16[128,512]{1,0:T(8,128)(2,1)S(1)}, u32[]{:S(2)}, u32[]{:S(2)}) %collective-permute-start.2) | collective-permute-done | bytes 131104 | tf_op jit(solution)/shard_map/ppermute | solution.py:25
  74.8 1.0 %fusion.28 = bf16[256,512]{1,0:T(8,128)(2,1)} fusion(f32[256,512]{1,0:T(8,128)S(1)} %fusion.51, bf16[512,512]{1,0:T(8,128)(2,1)S(1)} %copy-done, f32[512,512]{1,0:T(8,128)S(1)} %get-tuple-element.67, bf16[128,512]{1,0:T(8,128)(2,1)S(1)} %collective-permute-done.3, bf16[128,512]{1,0:T(8,128)(2,1)S(1)} %collective-permute-done.2), kind=kOutput, calls=%fused_computation.36 | convolution fusion | flops 135266304 | bytes 2097152 | tf_op jit(solution)/shard_map/dot_general | solution.py:128
  (24 shorter events, 0.5 us)
Async XLA Ops:
  0.6 25.2 %copy-start = (bf16[512,512]{1,0:T(8,128)(2,1)S(1)}, bf16[512,512]{1,0:T(8,128)(2,1)}, u32[]{:S(2)}) copy-start(bf16[512,512]{1,0:T(8,128)(2,1)} %param.19) | copy-start | bytes 1572868
  1.7 18.6 %collective-permute-start.1 = (bf16[128,512]{1,0:T(8,128)(2,1)S(1)}, bf16[128,512]{1,0:T(8,128)(2,1)S(1)}, u32[]{:S(2)}, u32[]{:S(2)}) collective-permute-start(bf16[128,512]{1,0:T(8,128)(2,1)S(1)} %get-tuple-element.115), channel_id=1, source_target_pairs={{1,0},{2,1},{3,2},{4,3},{5,4},{6,5},{7,6},{8,7},{9,8},{10,9},{11,1... | collective-permute-start | bytes 393224 | tf_op jit(solution)/shard_map/ppermute | solution.py:17
  15.3 10.6 %collective-permute-start = (bf16[128,512]{1,0:T(8,128)(2,1)S(1)}, bf16[128,512]{1,0:T(8,128)(2,1)}, u32[]{:S(2)}, u32[]{:S(2)}) collective-permute-start(bf16[128,512]{1,0:T(8,128)(2,1)S(1)} %get-tuple-element.114), channel_id=1, source_target_pairs={{0,1},{1,2},{2,3},{3,4},{4,5},{5,6},{6,7},{7,8},{8,9},{9,10},{10,1... | collective-permute-start | bytes 393224 | tf_op jit(solution)/shard_map/ppermute | solution.py:14
  34.0 1.0 %copy-start.3 = (bf16[256,8,128]{2,1,0:T(8,128)(2,1)S(1)}, bf16[256,8,128]{2,1,0:T(8,128)(2,1)}, u32[]{:S(2)}) copy-start(bf16[256,8,128]{2,1,0:T(8,128)(2,1)} %param.14) | copy-start | bytes 1572868
  34.0 1.1 %copy-start.5 = (bf16[128,512]{1,0:T(8,128)(2,1)S(1)}, bf16[128,512]{1,0:T(8,128)(2,1)}, u32[]{:S(2)}) copy-start(bf16[128,512]{1,0:T(8,128)(2,1)} %param.20) | copy-start | bytes 393220
  35.1 3.0 %copy-start.4 = (bf16[512,256]{1,0:T(8,128)(2,1)S(1)}, bf16[512,256]{1,0:T(8,128)(2,1)}, u32[]{:S(2)}) copy-start(bf16[512,256]{1,0:T(8,128)(2,1)} %param.21) | copy-start | bytes 786436
  35.1 5.3 %copy-start.2 = (bf16[256,8,256]{2,1,0:T(8,128)(2,1)S(1)}, bf16[256,8,256]{2,1,0:T(8,128)(2,1)}, u32[]{:S(2)}) copy-start(bf16[256,8,256]{2,1,0:T(8,128)(2,1)} %param.17) | copy-start | bytes 3145732
  49.1 17.3 %copy-start.1 = (bf16[512,512]{1,0:T(8,128)(2,1)S(1)}, bf16[512,512]{1,0:T(8,128)(2,1)}, u32[]{:S(2)}) copy-start(bf16[512,512]{1,0:T(8,128)(2,1)} %param.18) | copy-start | bytes 1572868
  62.0 4.8 %collective-permute-start.3 = (bf16[128,512]{1,0:T(8,128)(2,1)S(1)}, bf16[128,512]{1,0:T(8,128)(2,1)S(1)}, u32[]{:S(2)}, u32[]{:S(2)}) collective-permute-start(bf16[128,512]{1,0:T(8,128)(2,1)S(1)} %get-tuple-element.113), channel_id=1, source_target_pairs={{1,0},{2,1},{3,2},{4,3},{5,4},{6,5},{7,6},{8,7},{9,8},{10,9},{11,1... | collective-permute-start | bytes 393224 | tf_op jit(solution)/shard_map/ppermute | solution.py:25
  64.2 10.5 %collective-permute-start.2 = (bf16[128,512]{1,0:T(8,128)(2,1)S(1)}, bf16[128,512]{1,0:T(8,128)(2,1)S(1)}, u32[]{:S(2)}, u32[]{:S(2)}) collective-permute-start(bf16[128,512]{1,0:T(8,128)(2,1)S(1)} %get-tuple-element.112), channel_id=1, source_target_pairs={{0,1},{1,2},{2,3},{3,4},{4,5},{5,6},{6,7},{7,8},{8,9},{9,10},{10,1... | collective-permute-start | bytes 393224 | tf_op jit(solution)/shard_map/ppermute | solution.py:25
where the time goes:
time: 76.4 us; the launch traced here: 75.8 us
  matrix products  28.2 us (37%)
  starting transfers between devices  19.8 us (26%)
  waiting for transfers between devices  13.7 us (18%)
  local copies, waits for them, and re-layouts  8.63 us (11%)
  loops' own time  2.58 us (3%)
  other arithmetic  2.09 us (3%)
  between operations  0.82 us (1%)
    ppermute x1, starting transfers between devices, extended(): lax.ppermute(lax.slice_in_dim(block, 0, width, axis=dim), axis, backward)  13.6 us
    ppermute x2, waiting for transfers between devices, shifted(): lax.ppermute(value, axis, [(source, source + steps) for source in range(i...  8.1 us
    ppermute x1, waiting for transfers between devices, extended(): lax.ppermute(lax.slice_in_dim(block, block.shape[dim] - width, None, axis...  5.6 us
    dot_general x2, matrix products, one_block(): lax.dot_general(picker, high, contract, preferred_element_type=jnp.float32)  5.12 us
    dot_general x2, matrix products, one_block(): lax.dot_general(picker, low, contract, preferred_element_type=jnp.float32)  5.08 us
    mul x1, local copies, waits for them, and re-layouts, body(): d_message * live_mask  4.38 us
    ppermute x2, starting transfers between devices, shifted(): lax.ppermute(value, axis, [(source, source + steps) for source in range(i...  4.33 us
    dot_general x1, matrix products, body(): jnp.dot(cotangent.reshape(-1, block_width), w_block.T, preferred_element_...  4.12 us
  transfers between devices with their start and end apart: 4, of which 3 were waited for; matrix products, arithmetic and copies ran while one was open for 4% of the time, Pallas kernels for 0%

commit v1 on v0

v1 whole, which is shorter than its diff:
```python
import functools

import jax
import jax.numpy as jnp
from jax import lax
from jax.experimental import pallas as pl
from jax.experimental.pallas import tpu as pltpu
from jax.sharding import PartitionSpec as P

MESH = pl.DeviceIdType.MESH
BF = jnp.bfloat16
F32 = jnp.float32
DEAD = 1024.0
NT = (((1,), (1,)), ((), ()))


def dot(a, b):
    return jnp.dot(a, b, preferred_element_type=F32)


def dot_nt(a, b):
    return lax.dot_general(a, b, NT, preferred_element_type=F32)


def hot(mask):
    return jnp.where(mask, 1.0, 0.0).astype(BF)


def kernel(
    n_dev, slots, half, chunk,
    feat_hbm, rad_hbm, nbr_hbm, cnt_hbm, cot_hbm, ws_hbm, wn_hbm, wr_hbm, wb_hbm,
    blk_hbm, fg_hbm,
    feat, rad, nbr, cnt, cot, ws, wn, wr, wb,
    halo, rim_out, rim_in, own_proj, mix, p_own, p_rim, pt_own, pt_rim,
    gate, had, u_own, msg, adj, blk, own_sum, self_adj, fg_self, fg,
    in_sem, halo_send, halo_recv, rim_send, rim_recv, blk_sem, fg_sem,
):
    me = lax.axis_index("cell")
    right, left = lax.rem(me + 1, n_dev), lax.rem(me + n_dev - 1, n_dev)
    edges = half * slots

    barrier = pltpu.get_barrier_semaphore()
    for other in (left, right):
        pl.semaphore_signal(barrier, inc=1, device_id=(other,), device_id_type=MESH)

    pairs = [(nbr_hbm, nbr), (cnt_hbm, cnt), (feat_hbm, feat), (wn_hbm, wn), (ws_hbm, ws),
             (rad_hbm, rad), (wr_hbm, wr), (cot_hbm, cot), (wb_hbm, wb)]
    loads = [pltpu.make_async_copy(s, d, in_sem.at[i]) for i, (s, d) in enumerate(pairs)]
    for load in loads:
        load.start()

    pl.semaphore_wait(barrier, 2)
    halo_copies = [
        pltpu.make_async_remote_copy(
            src_ref=feat_hbm.at[pl.ds((1 - side) * half, half)], dst_ref=halo.at[side],
            send_sem=halo_send.at[side], recv_sem=halo_recv.at[side],
            device_id=((right, left)[side],), device_id_type=MESH)
        for side in (0, 1)
    ]
    for copy in halo_copies:
        copy.start()

    loads[0].wait()
    loads[1].wait()
    e_row = lax.broadcasted_iota(jnp.int32, (edges, half), 0)
    lane = lax.broadcasted_iota(jnp.int32, (edges, half), 1)
    spread = hot((e_row // slots) == lane)
    slot_of = lax.broadcasted_iota(jnp.int32, (slots, edges), 1)
    atom_lane = (slot_of // slots).astype(F32)
    slot_of = slot_of % slots
    slot_sub = lax.broadcasted_iota(jnp.int32, (slots, edges), 0)
    slot_pick = slot_of == slot_sub
    for h in (0, 1):
        ids = nbr[:, h * half:(h + 1) * half]
        shape = (slots, half)
        base = me * (2 * half) + h * half
        diff = ids - base - lax.broadcasted_iota(jnp.int32, shape, 1)
        live = lax.broadcasted_iota(jnp.int32, shape, 0) < cnt[:, h * half:(h + 1) * half]
        diff = jnp.where(live, diff.astype(F32), DEAD).astype(BF)
        z = jnp.where(slot_pick, dot_nt(diff, spread), 0.0)
        row = jnp.sum(z, axis=0, keepdims=True)
        row_t = row + atom_lane[:1] + half
        row_self = jnp.where(row < DEAD / 2, atom_lane[:1], -1.0)
        own_js = (1, 2) if h == 0 else (0, 1)
        rim_j = 0 if h == 0 else 2
        for c in range(0, edges, chunk):
            sub = lax.broadcasted_iota(jnp.int32, (half, chunk), 0).astype(F32)
            rt = row_t[:, c:c + chunk]
            rs = row_self[:, c:c + chunk]
            for pos, j in enumerate(own_js):
                pt_own[pos * half:(pos + 1) * half, h * edges + c:h * edges + c + chunk] = hot(
                    sub + j * half == rt)
            pt_rim[h, 0:half, c:c + chunk] = hot(sub + rim_j * half == rt)
            pt_rim[h, half:2 * half, c:c + chunk] = hot(sub == rs)
        for c in range(0, edges, chunk):
            part = spread[c:c + chunk]
            y = dot_nt(part, diff)
            r8 = lax.broadcasted_iota(jnp.int32, (chunk, slots), 0) % slots
            l8 = lax.broadcasted_iota(jnp.int32, (chunk, slots), 1)
            y = jnp.where(r8 == l8, y, 0.0).astype(BF)
            b = dot(y, jnp.ones((slots, half), BF))
            atom = ((lax.broadcasted_iota(jnp.int32, (chunk, half), 0) + c) // slots).astype(F32)
            col = lax.broadcasted_iota(jnp.int32, (chunk, half), 1).astype(F32)
            ct = b + atom + half
            cs = jnp.where(b < DEAD / 2, atom, -1.0)
            r0 = h * edges + c
            for pos, j in enumerate(own_js):
                p_own[r0:r0 + chunk, pos * half:(pos + 1) * half] = hot(col + j * half == ct)
            p_rim[r0:r0 + chunk, 0:half] = hot(col + rim_j * half == ct)
            p_rim[r0:r0 + chunk, half:2 * half] = hot(col == cs)

    for i in (2, 3, 4):
        loads[i].wait()
    own_proj[...] = dot(feat[...], wn[...]).astype(BF)
    for h in (0, 1):
        mix[h, half:2 * half] = dot(feat[h * half:(h + 1) * half], ws[...]).astype(BF)

    for i in (5, 6, 7, 8):
        loads[i].wait()

    @pl.loop(0, 2 * edges // chunk)
    def _(i):
        rows = pl.ds(pl.multiple_of(i * chunk, chunk), chunk)
        g = 0.5 * dot(rad[rows], wr[...])
        gate[rows] = g
        had[rows] = dot_nt(cot[rows], wb[...]) * g
        u_own[rows] = dot(p_own[rows], own_proj[...])

    rim_copies = []
    for h in (0, 1):
        halo_copies[h].wait_recv()
        mix[h, 0:half] = dot(halo[h], wn[...]).astype(BF)

        @pl.loop(0, edges // chunk)
        def _(i):
            rows = pl.ds(pl.multiple_of(h * edges + i * chunk, chunk), chunk)
            u = u_own[rows] + dot(p_rim[rows], mix[h])
            p = u * gate[rows]
            t = jnp.tanh(p)
            pt = p * t
            msg[rows] = (p + pt).astype(BF)
            adj[rows] = (had[rows] * ((1.0 + t) * ((1.0 + p) - pt))).astype(BF)

        here = adj.at[pl.ds(h * edges, edges)]
        rim_out[h] = dot(pt_rim[h, 0:half], here[...]).astype(BF)
        copy = pltpu.make_async_remote_copy(
            src_ref=rim_out.at[h], dst_ref=rim_in.at[h],
            send_sem=rim_send.at[h], recv_sem=rim_recv.at[h],
            device_id=((left, right)[h],), device_id_type=MESH)
        copy.start()
        rim_copies.append(copy)

    blk_copies = []
    for c in range(2):
        @pl.loop(0, edges // chunk)
        def _(i):
            rows = pl.ds(pl.multiple_of(c * edges + i * chunk, chunk), chunk)
            blk[rows] = dot(msg[rows], wb[...]).astype(BF)

        part = pl.ds(c * edges, edges)
        copy = pltpu.make_async_copy(blk.at[part], blk_hbm.at[part], blk_sem.at[c])
        copy.start()
        blk_copies.append(copy)

    own_sum[...] = dot(pt_own[...], adj[...])
    for h in (0, 1):
        self_adj[h * half:(h + 1) * half] = dot(
            pt_rim[h, half:2 * half], adj[h * edges:(h + 1) * edges]).astype(BF)
    fg_self[...] = dot_nt(self_adj[...], ws[...])

    fg_copies = []
    for h in (0, 1):
        rim_copies[h].wait_recv()
        rows = pl.ds((1 - h) * half, half)
        total = (own_sum[rows] + rim_in[h].astype(F32)).astype(BF)
        fg[rows] = (fg_self[rows] + dot_nt(total, wn[...])).astype(BF)
        copy = pltpu.make_async_copy(fg.at[rows], fg_hbm.at[rows], fg_sem.at[h])
        copy.start()
        fg_copies.append(copy)

    for copy in blk_copies + fg_copies:
        copy.wait()
    for copy in halo_copies + rim_copies:
        copy.wait_send()


def body(features, radial, neighbours, counts, cotangent, w_self, w_neighbour, w_radial, w_block):
    atoms, width = features.shape
    slots = neighbours.shape[1]
    basis = radial.shape[2]
    out_width = w_block.shape[1]
    half = atoms // 2
    edges = atoms * slots
    n_dev = lax.axis_size("cell")
    any_spec = pl.BlockSpec(memory_space=pl.ANY)
    vm = pltpu.VMEM
    dma = pltpu.SemaphoreType.DMA
    blocks, grad = pl.pallas_call(
        functools.partial(kernel, n_dev, slots, half, 256),
        name="edge_layer",
        out_shape=(
            jax.ShapeDtypeStruct((edges, out_width), BF),
            jax.ShapeDtypeStruct((atoms, width), BF),
        ),
        in_specs=[any_spec] * 9,
        out_specs=(any_spec, any_spec),
        scratch_shapes=[
            vm((atoms, width), BF), vm((edges, basis), BF), vm((slots, atoms), jnp.int32),
            vm((1, atoms), jnp.int32), vm((edges, out_width), BF), vm((width, width), BF),
            vm((width, width), BF), vm((basis, width), BF), vm((width, out_width), BF),
            vm((2, half, width), BF), vm((2, half, width), BF), vm((2, half, width), BF),
            vm((atoms, width), BF), vm((2, 2 * half, width), BF),
            vm((edges, atoms), BF), vm((edges, atoms), BF),
            vm((atoms, edges), BF), vm((2, atoms, edges // 2), BF),
            vm((edges, width), F32), vm((edges, width), F32), vm((edges, width), F32),
            vm((edges, width), BF), vm((edges, width), BF), vm((edges, out_width), BF),
            vm((atoms, width), F32), vm((atoms, width), BF), vm((atoms, width), F32),
            vm((atoms, width), BF),
            dma((9,)), dma((2,)), dma((2,)), dma((2,)), dma((2,)), dma((2,)), dma((2,)),
        ],
        compiler_params=pltpu.CompilerParams(
            collective_id=0, has_side_effects=True, vmem_limit_bytes=56 * 1024 * 1024),
    )(
        features, radial.reshape(edges, basis), neighbours.T, counts.reshape(1, atoms),
        cotangent.reshape(edges, out_width), w_self, w_neighbour, w_radial, w_block,
    )
    return blocks.reshape(atoms, slots, out_width), grad


def solution(mesh):
    in_specs = (
        P("cell", None),
        P("cell", None, None),
        P("cell", None),
        P("cell"),
        P("cell", None, None),
        P(),
        P(),
        P(),
        P(),
    )
    out_specs = (P("cell", None, None), P("cell", None))
    return jax.shard_map(body, mesh=mesh, in_specs=in_specs, out_specs=out_specs, check_vma=False)
```

time: 76.4 us -> 30.8 us (0.40)
  matrix products: 28.2 us -> 0 us
  Pallas kernels: 0 us -> 27 us
  starting transfers between devices: 19.8 us -> 0 us
  waiting for transfers between devices: 13.7 us -> 0 us
  local copies, waits for them, and re-layouts: 8.63 us -> 3.01 us
  loops' own time: 2.58 us -> 0 us
  other arithmetic: 2.09 us -> 0 us
    dot_general x13 -> x0, matrix products: 28.2 us -> none  [the longest x2 5.12 us: one_block(): lax.dot_general(picker, high, contract, preferred_element_type=jnp.float32)]
    pallas_call x0 -> x1, Pallas kernels: none -> 27 us  [body(): pl.pallas_call(functools.partial(kernel, n_dev, slots, half, 256), name='...]
    ppermute x4 -> x0, starting transfers between devices: 19.8 us -> none  [the longest x1 13.6 us: extended(): lax.ppermute(lax.slice_in_dim(block, 0, width, axis=dim), axis, backward)]
    ppermute x4 -> x0, waiting for transfers between devices: 13.7 us -> none  [the longest x2 8.1 us: shifted(): lax.ppermute(value, axis, [(source, source + steps) for source in range(i...]
    mul x1 -> x0, local copies, waits for them, and re-layouts: 4.38 us -> none  [body(): d_message * live_mask]
    another operation x2 -> x0, loops' own time: 2.58 us -> none  [the longest x1 1.38 us: window_add(): lax.scan(one_block, start_sum, (jnp.arange(block_total, dtype=jnp.int32),...]
    unnamed x12 -> x4, local copies, waits for them, and re-layouts: 0.48 us -> 3.01 us
    dynamic_slice x4 -> x0, local copies, waits for them, and re-layouts: 2.35 us -> none  [window_pick(): lax.map(one_block, (jnp.arange(block_total, dtype=jnp.int32), grouped))]
  transfers between devices with their start and end apart: 4 -> 0, of which waited for: 3 -> 0; matrix products, arithmetic and copies ran while one was open for 4% -> 0% of each run, Pallas kernels for 0% -> 0%
where the time goes in v1:
time: 30.8 us; the launch traced here: 30.7 us
  Pallas kernels  27 us (88%)
  local copies, waits for them, and re-layouts  3.01 us (10%)
  between operations  0.65 us (2%)
    pallas_call x1, Pallas kernels, body(): pl.pallas_call(functools.partial(kernel, n_dev, slots, half, 256), name='...  27 us
    unnamed x4, local copies, waits for them, and re-layouts  3.01 us

profile of v1, /device:TPU:6, one launch (start us, length us, event | category | flops | bytes accessed | tf_op | source)
XLA Modules:
  0.0 30.7 jit_solution(2673578790524311920)
XLA Ops:
  0.6 27.0 %edge_layer.1 = (bf16[2048,256]{1,0:T(8,128)(2,1)}, bf16[256,512]{1,0:T(8,128)(2,1)}) custom-call(bf16[256,512]{1,0:T(8,128)(2,1)} %feat_hbm.1, bf16[2048,128]{1,0:T(8,128)(2,1)} %bitcast.7, s32[8,256]{1,0:T(8,128)} %bitcast.8, s32[1,256]{1,0:T(1,128)} %bitcast.9, bf16[2048,256]{1,0:T(8,128)(2,1)} %bitcast.5, bf16[512,512]{1,0:T(8,128)(2,1)} %ws_hbm.1, ...), custom_call_target="tpu_custom_call" | custom-call | tf_op jit(solution)/shard_map/edge_layer/pallas_call | solution.py:198
  27.6 0.0 copy-start
  27.6 2.3 %copy.13 = bf16[256,8,256]{2,1,0:T(8,128)(2,1)} copy(bf16[256,8,256]{2,1,0:T(8,128)(2,1)} %bitcast.6) | data formatting | bytes 2097152
  30.0 0.0 copy-done
  30.0 0.7 %copy.14 = bf16[256,512]{1,0:T(8,128)(2,1)} copy(bf16[256,512]{1,0:T(8,128)(2,1)S(1)} %copy-done) | data formatting | bytes 524288
Async XLA Ops:
  27.6 2.3 %copy-start = (bf16[256,512]{1,0:T(8,128)(2,1)S(1)}, bf16[256,512]{1,0:T(8,128)(2,1)}, u32[]{:S(2)}) copy-start(bf16[256,512]{1,0:T(8,128)(2,1)} %get-tuple-element.9) | copy-start | bytes 786436

commit v2 on v1

--- a/solution.py
+++ b/solution.py
@@ -29,19 +29,23 @@
 def kernel(
     n_dev, slots, half, chunk,
     feat_hbm, rad_hbm, nbr_hbm, cnt_hbm, cot_hbm, ws_hbm, wn_hbm, wr_hbm, wb_hbm,
-    blk_hbm, fg_hbm,
+    blk, fg,
     feat, rad, nbr, cnt, cot, ws, wn, wr, wb,
     halo, rim_out, rim_in, own_proj, mix, p_own, p_rim, pt_own, pt_rim,
-    gate, had, u_own, msg, adj, blk, own_sum, self_adj, fg_self, fg,
-    in_sem, halo_send, halo_recv, rim_send, rim_recv, blk_sem, fg_sem,
+    gate, had, u_own, msg, adj, own_sum, self_adj, fg_self,
+    in_sem, halo_send, halo_recv, rim_send, rim_recv,
 ):
     me = lax.axis_index("cell")
-    right, left = lax.rem(me + 1, n_dev), lax.rem(me + n_dev - 1, n_dev)
     edges = half * slots
 
+    has = (me > 0, me < n_dev - 1)
+    peer = (me - 1, me + 1)
+
     barrier = pltpu.get_barrier_semaphore()
-    for other in (left, right):
-        pl.semaphore_signal(barrier, inc=1, device_id=(other,), device_id_type=MESH)
+    for side in (0, 1):
+        @pl.when(has[side])
+        def _():
+            pl.semaphore_signal(barrier, inc=1, device_id=(peer[side],), device_id_type=MESH)
 
     pairs = [(nbr_hbm, nbr), (cnt_hbm, cnt), (feat_hbm, feat), (wn_hbm, wn), (ws_hbm, ws),
              (rad_hbm, rad), (wr_hbm, wr), (cot_hbm, cot), (wb_hbm, wb)]
@@ -49,16 +53,31 @@
     for load in loads:
         load.start()
 
-    pl.semaphore_wait(barrier, 2)
+    pl.semaphore_wait(barrier, has[0].astype(jnp.int32) + has[1].astype(jnp.int32))
+
     halo_copies = [
         pltpu.make_async_remote_copy(
-            src_ref=feat_hbm.at[pl.ds((1 - side) * half, half)], dst_ref=halo.at[side],
-            send_sem=halo_send.at[side], recv_sem=halo_recv.at[side],
-            device_id=((right, left)[side],), device_id_type=MESH)
+            src_ref=feat_hbm.at[pl.ds(side * half, half)], dst_ref=halo.at[1 - side],
+            send_sem=halo_send.at[side], recv_sem=halo_recv.at[1 - side],
+            device_id=(peer[side],), device_id_type=MESH)
         for side in (0, 1)
     ]
-    for copy in halo_copies:
-        copy.start()
+    rim_copies = [
+        pltpu.make_async_remote_copy(
+            src_ref=rim_out.at[side], dst_ref=rim_in.at[1 - side],
+            send_sem=rim_send.at[side], recv_sem=rim_recv.at[1 - side],
+            device_id=(peer[side],), device_id_type=MESH)
+        for side in (0, 1)
+    ]
+    for side in (0, 1):
+        @pl.when(has[side])
+        def _():
+            halo_copies[side].start()
+
+        @pl.when(jnp.logical_not(has[side]))
+        def _():
+            halo[side] = jnp.zeros_like(halo[side])
+            rim_in[side] = jnp.zeros_like(rim_in[side])
 
     loads[0].wait()
     loads[1].wait()
@@ -118,7 +137,7 @@
     for i in (5, 6, 7, 8):
         loads[i].wait()
 
-    @pl.loop(0, 2 * edges // chunk)
+    @pl.loop(0, 2 * edges // chunk, unroll=True)
     def _(i):
         rows = pl.ds(pl.multiple_of(i * chunk, chunk), chunk)
         g = 0.5 * dot(rad[rows], wr[...])
@@ -126,12 +145,14 @@
         had[rows] = dot_nt(cot[rows], wb[...]) * g
         u_own[rows] = dot(p_own[rows], own_proj[...])
 
-    rim_copies = []
-    for h in (0, 1):
-        halo_copies[h].wait_recv()
+    for h in (1, 0):
+        @pl.when(has[h])
+        def _():
+            halo_copies[1 - h].wait_recv()
+
         mix[h, 0:half] = dot(halo[h], wn[...]).astype(BF)
 
-        @pl.loop(0, edges // chunk)
+        @pl.loop(0, edges // chunk, unroll=True)
         def _(i):
             rows = pl.ds(pl.multiple_of(h * edges + i * chunk, chunk), chunk)
             u = u_own[rows] + dot(p_rim[rows], mix[h])
@@ -143,45 +164,45 @@
 
         here = adj.at[pl.ds(h * edges, edges)]
         rim_out[h] = dot(pt_rim[h, 0:half], here[...]).astype(BF)
-        copy = pltpu.make_async_remote_copy(
-            src_ref=rim_out.at[h], dst_ref=rim_in.at[h],
-            send_sem=rim_send.at[h], recv_sem=rim_recv.at[h],
-            device_id=((left, right)[h],), device_id_type=MESH)
-        copy.start()
-        rim_copies.append(copy)
-
-    blk_copies = []
+
+        @pl.when(has[h])
+        def _():
+            rim_copies[h].start()
+
     for c in range(2):
-        @pl.loop(0, edges // chunk)
+        @pl.loop(0, edges // chunk, unroll=True)
         def _(i):
             rows = pl.ds(pl.multiple_of(c * edges + i * chunk, chunk), chunk)
             blk[rows] = dot(msg[rows], wb[...]).astype(BF)
 
-        part = pl.ds(c * edges, edges)
-        copy = pltpu.make_async_copy(blk.at[part], blk_hbm.at[part], blk_sem.at[c])
-        copy.start()
-        blk_copies.append(copy)
-
     own_sum[...] = dot(pt_own[...], adj[...])
     for h in (0, 1):
         self_adj[h * half:(h + 1) * half] = dot(
             pt_rim[h, half:2 * half], adj[h * edges:(h + 1) * edges]).astype(BF)
     fg_self[...] = dot_nt(self_adj[...], ws[...])
 
-    fg_copies = []
-    for h in (0, 1):
-        rim_copies[h].wait_recv()
-        rows = pl.ds((1 - h) * half, half)
+    for h in (0, 1):
+        @pl.when(has[h])
+        def _():
+            rim_copies[1 - h].wait_recv()
+
+        rows = pl.ds(h * half, half)
         total = (own_sum[rows] + rim_in[h].astype(F32)).astype(BF)
         fg[rows] = (fg_self[rows] + dot_nt(total, wn[...])).astype(BF)
-        copy = pltpu.make_async_copy(fg.at[rows], fg_hbm.at[rows], fg_sem.at[h])
+
+    for side in (0, 1):
+        @pl.when(has[side])
+        def _():
+            halo_copies[side].wait_send()
+            rim_copies[side].wait_send()
+
+
+def store_kernel(blk, fg, blk_hbm, fg_hbm, sem):
+    copies = [pltpu.make_async_copy(blk, blk_hbm, sem.at[0]), pltpu.make_async_copy(fg, fg_hbm, sem.at[1])]
+    for copy in copies:
         copy.start()
-        fg_copies.append(copy)
-
-    for copy in blk_copies + fg_copies:
+    for copy in copies:
         copy.wait()
-    for copy in halo_copies + rim_copies:
-        copy.wait_send()
 
 
 def body(features, radial, neighbours, counts, cotangent, w_self, w_neighbour, w_radial, w_block):
@@ -199,11 +220,11 @@
         functools.partial(kernel, n_dev, slots, half, 256),
         name="edge_layer",
         out_shape=(
-            jax.ShapeDtypeStruct((edges, out_width), BF),
-            jax.ShapeDtypeStruct((atoms, width), BF),
+            vm((edges, out_width), BF),
+            vm((atoms, width), BF),
         ),
         in_specs=[any_spec] * 9,
-        out_specs=(any_spec, any_spec),
+        out_specs=(pl.BlockSpec(memory_space=vm),) * 2,
         scratch_shapes=[
             vm((atoms, width), BF), vm((edges, basis), BF), vm((slots, atoms), jnp.int32),
             vm((1, atoms), jnp.int32), vm((edges, out_width), BF), vm((width, width), BF),
@@ -213,10 +234,9 @@
             vm((edges, atoms), BF), vm((edges, atoms), BF),
             vm((atoms, edges), BF), vm((2, atoms, edges // 2), BF),
             vm((edges, width), F32), vm((edges, width), F32), vm((edges, width), F32),
-            vm((edges, width), BF), vm((edges, width), BF), vm((edges, out_width), BF),
+            vm((edges, width), BF), vm((edges, width), BF),
             vm((atoms, width), F32), vm((atoms, width), BF), vm((atoms, width), F32),
-            vm((atoms, width), BF),
-            dma((9,)), dma((2,)), dma((2,)), dma((2,)), dma((2,)), dma((2,)), dma((2,)),
+            dma((9,)), dma((2,)), dma((2,)), dma((2,)), dma((2,)),
         ],
         compiler_params=pltpu.CompilerParams(
             collective_id=0, has_side_effects=True, vmem_limit_bytes=56 * 1024 * 1024),
@@ -224,6 +244,17 @@
         features, radial.reshape(edges, basis), neighbours.T, counts.reshape(1, atoms),
         cotangent.reshape(edges, out_width), w_self, w_neighbour, w_radial, w_block,
     )
+    blocks, grad = pl.pallas_call(
+        store_kernel,
+        name="store",
+        out_shape=(
+            jax.ShapeDtypeStruct((edges, out_width), BF),
+            jax.ShapeDtypeStruct((atoms, width), BF),
+        ),
+        in_specs=[pl.BlockSpec(memory_space=vm)] * 2,
+        out_specs=(any_spec, any_spec),
+        scratch_shapes=[dma((2,))],
+    )(pltpu.with_memory_space_constraint(blocks, pltpu.VMEM), pltpu.with_memory_space_constraint(grad, pltpu.VMEM))
     return blocks.reshape(atoms, slots, out_width), grad
 
 

time: 30.8 us -> 27.8 us (0.903)
  local copies, waits for them, and re-layouts: 3.01 us -> 0 us
    unnamed x4 -> x0, local copies, waits for them, and re-layouts: 3.01 us -> none
    pallas_call x1, Pallas kernels: 27 us -> 25.9 us  [body(): pl.pallas_call(functools.partial(kernel, n_dev, slots, half, 256), name='...]
    pallas_call x0 -> x1, Pallas kernels: none -> 1.07 us  [body(): pl.pallas_call(store_kernel, name='store', out_shape=(jax.ShapeDtypeStruc...]
where the time goes in v2:
time: 27.8 us; the launch traced here: 27.6 us
  Pallas kernels  27 us (97%)
  between operations  0.64 us (2%)
    pallas_call x1, Pallas kernels, body(): pl.pallas_call(functools.partial(kernel, n_dev, slots, half, 256), name='...  25.9 us
    pallas_call x1, Pallas kernels, body(): pl.pallas_call(store_kernel, name='store', out_shape=(jax.ShapeDtypeStruc...  1.07 us

profile of v2, /device:TPU:6, one launch (start us, length us, event | category | flops | bytes accessed | tf_op | source)
XLA Modules:
  0.0 27.6 jit_solution(4060559628993873212)
XLA Ops:
  0.6 25.9 %edge_layer.1 = (bf16[2048,256]{1,0:T(8,128)(2,1)S(1)}, bf16[256,512]{1,0:T(8,128)(2,1)S(1)}) custom-call(bf16[256,512]{1,0:T(8,128)(2,1)} %feat_hbm.1, bf16[2048,128]{1,0:T(8,128)(2,1)} %bitcast.6, s32[8,256]{1,0:T(8,128)} %bitcast.7, s32[1,256]{1,0:T(1,128)} %bitcast.8, bf16[2048,256]{1,0:T(8,128)(2,1)} %bitcast.5, bf16[512,512]{1,0:T(8,128)(2,1)} %ws_hbm.1, ...), custom_call_target="tpu_custom_call" | custom-call | tf_op jit(solution)/shard_map/edge_layer/pallas_call | solution.py:219
  26.5 1.1 %store.1 = (bf16[2048,256]{1,0:T(8,128)(2,1)}, bf16[256,512]{1,0:T(8,128)(2,1)}) custom-call(bf16[2048,256]{1,0:T(8,128)(2,1)S(1)} %get-tuple-element.6.blk, bf16[256,512]{1,0:T(8,128)(2,1)S(1)} %get-tuple-element.7.fg), custom_call_target="tpu_custom_call" | custom-call | tf_op jit(solution)/shard_map/store/pallas_call | solution.py:247

commit v3 on v2

v3 whole, which is shorter than its diff:
```python
import functools

import jax
import jax.numpy as jnp
from jax import lax
from jax.experimental import pallas as pl
from jax.experimental.pallas import tpu as pltpu
from jax.sharding import PartitionSpec as P

MESH = pl.DeviceIdType.MESH
BF = jnp.bfloat16
F32 = jnp.float32
DEAD = 1024.0
COLS = 2
ROUND = 128
RELAY = 14
NT = (((1,), (1,)), ((), ()))


def dot(a, b):
    return jnp.dot(a, b, preferred_element_type=F32)


def dot_nt(a, b):
    return lax.dot_general(a, b, NT, preferred_element_type=F32)


def hot(mask):
    return jnp.where(mask, 1.0, 0.0).astype(BF)


def kernel(
    n_dev, slots, half, chunk,
    feat_hbm, rad_hbm, nbr_hbm, cnt_hbm, cot_hbm, ws_hbm, wn_hbm, wr_hbm, wb_hbm,
    blk, fg,
    feat, rad, nbr, cnt, cot, ws, wn, wr, wb,
    halo, passed, rim_out, rim_in, proj, p_own, p_rim, pt_own, pt_rim, pt_self,
    gate, had, u_own, msg, adj, own_sum, fg_self,
    in_sem, halo_send, halo_recv, pass_send, pass_recv, rim_send, rim_recv,
):
    me = lax.axis_index("cell")
    has = (me > 0, me < n_dev - 1)
    peer = (me - 1, me + 1)
    spot = lax.rem(me, ROUND)
    far_low = jnp.logical_and(spot == ROUND - 1, has[1])
    far_high = jnp.logical_and(spot == 0, has[0])
    relay = jnp.logical_and(spot == RELAY, me + ROUND < n_dev)
    greet = (me - 1, jnp.where(far_low, me - (ROUND - 1 - RELAY), me + 1))
    edges = half * slots
    width = feat.shape[1]
    part = width // COLS

    barrier = pltpu.get_barrier_semaphore()
    for side in (0, 1):
        @pl.when(has[side])
        def _():
            pl.semaphore_signal(barrier, inc=1, device_id=(greet[side],), device_id_type=MESH)

    @pl.when(relay)
    def _():
        pl.semaphore_signal(
            barrier, inc=1, device_id=(me + ROUND - RELAY,), device_id_type=MESH)

    pairs = [(feat_hbm, feat), (wn_hbm, wn), (nbr_hbm, nbr), (cnt_hbm, cnt), (ws_hbm, ws),
             (rad_hbm, rad), (wr_hbm, wr), (cot_hbm, cot), (wb_hbm, wb)]
    loads = [pltpu.make_async_copy(s, d, in_sem.at[i]) for i, (s, d) in enumerate(pairs)]
    for load in loads:
        load.start()

    loads[0].wait()
    loads[1].wait()
    own = dot(feat[...], wn[...]).astype(BF)
    for h in (0, 1):
        proj[h, 0:2 * half] = own

    halo_copies = [[
        pltpu.make_async_remote_copy(
            src_ref=proj.at[0, pl.ds(side * half, half), pl.ds(c * part, part)],
            dst_ref=halo.at[1 - side, c],
            send_sem=halo_send.at[side, c], recv_sem=halo_recv.at[1 - side, c],
            device_id=(peer[side],), device_id_type=MESH)
        for c in range(COLS)] for side in (0, 1)]
    rim_copies = [[
        pltpu.make_async_remote_copy(
            src_ref=rim_out.at[side, c], dst_ref=rim_in.at[1 - side, c],
            send_sem=rim_send.at[side, c], recv_sem=rim_recv.at[1 - side, c],
            device_id=(peer[side],), device_id_type=MESH)
        for c in range(COLS)] for side in (0, 1)]

    pass_in = [
        pltpu.make_async_remote_copy(
            src_ref=proj.at[0, pl.ds(0, half), pl.ds(c * part, part)], dst_ref=passed.at[c],
            send_sem=halo_send.at[0, c], recv_sem=pass_recv.at[c],
            device_id=(me - (ROUND - RELAY),), device_id_type=MESH)
        for c in range(COLS)]
    pass_on = [
        pltpu.make_async_remote_copy(
            src_ref=passed.at[c], dst_ref=halo.at[1, c],
            send_sem=pass_send.at[c], recv_sem=halo_recv.at[1, c],
            device_id=(me + (ROUND - 1 - RELAY),), device_id_type=MESH)
        for c in range(COLS)]

    def meet():
        count = has[0].astype(jnp.int32) + has[1].astype(jnp.int32) + relay.astype(jnp.int32)
        pl.semaphore_wait(barrier, count)

        @pl.when(far_high)
        def _():
            for copy in pass_in:
                copy.start()

        @pl.when(jnp.logical_and(has[0], jnp.logical_not(far_high)))
        def _():
            for copy in halo_copies[0]:
                copy.start()

        @pl.when(has[1])
        def _():
            for copy in halo_copies[1]:
                copy.start()

    @pl.when(jnp.logical_not(relay))
    def _():
        meet()

    for side in (0, 1):
        @pl.when(jnp.logical_not(has[side]))
        def _():
            halo[side] = jnp.zeros_like(halo[side])
            rim_in[side] = jnp.zeros_like(rim_in[side])

    loads[2].wait()
    loads[3].wait()
    e_row = lax.broadcasted_iota(jnp.int32, (edges, half), 0)
    lane = lax.broadcasted_iota(jnp.int32, (edges, half), 1)
    spread = hot((e_row // slots) == lane)
    slot_of = lax.broadcasted_iota(jnp.int32, (slots, edges), 1)
    atom_lane = (slot_of // slots).astype(F32)
    slot_of = slot_of % slots
    slot_sub = lax.broadcasted_iota(jnp.int32, (slots, edges), 0)
    slot_pick = slot_of == slot_sub
    for h in (1, 0):
        ids = nbr[:, h * half:(h + 1) * half]
        shape = (slots, half)
        base = me * (2 * half) + h * half
        diff = ids - base - lax.broadcasted_iota(jnp.int32, shape, 1)
        live = lax.broadcasted_iota(jnp.int32, shape, 0) < cnt[:, h * half:(h + 1) * half]
        diff = jnp.where(live, diff.astype(F32), DEAD).astype(BF)
        z = jnp.where(slot_pick, dot_nt(diff, spread), 0.0)
        row = jnp.sum(z, axis=0, keepdims=True)
        row_t = row + atom_lane[:1] + half
        row_self = jnp.where(row < DEAD / 2, atom_lane[:1], -1.0)
        own_js = (1, 2) if h == 0 else (0, 1)
        rim_j = 0 if h == 0 else 2
        for c in range(0, edges, chunk):
            sub = lax.broadcasted_iota(jnp.int32, (half, chunk), 0).astype(F32)
            rt = row_t[:, c:c + chunk]
            rs = row_self[:, c:c + chunk]
            for pos, j in enumerate(own_js):
                pt_own[pos * half:(pos + 1) * half, h * edges + c:h * edges + c + chunk] = hot(
                    sub + j * half == rt)
            pt_rim[h, :, c:c + chunk] = hot(sub + rim_j * half == rt)
            pt_self[h, :, c:c + chunk] = hot(sub == rs)
        for c in range(0, edges, chunk):
            y = dot_nt(spread[c:c + chunk], diff)
            r8 = lax.broadcasted_iota(jnp.int32, (chunk, slots), 0) % slots
            l8 = lax.broadcasted_iota(jnp.int32, (chunk, slots), 1)
            y = jnp.where(r8 == l8, y, 0.0).astype(BF)
            b = dot(y, jnp.ones((slots, half), BF))
            atom = ((lax.broadcasted_iota(jnp.int32, (chunk, half), 0) + c) // slots).astype(F32)
            col = lax.broadcasted_iota(jnp.int32, (chunk, half), 1).astype(F32)
            ct = b + atom + half
            cs = jnp.where(b < DEAD / 2, atom, -1.0)
            rows = slice(h * edges + c, h * edges + c + chunk)
            for pos, j in enumerate(own_js):
                p_own[rows, pos * half:(pos + 1) * half] = hot(col + j * half == ct)
            p_own[rows, 2 * half:3 * half] = hot(col == cs)
            p_rim[rows] = hot(col + rim_j * half == ct)

    loads[4].wait()
    for h in (0, 1):
        proj[h, 2 * half:3 * half] = dot(feat[h * half:(h + 1) * half], ws[...]).astype(BF)

    for i in (5, 6, 7, 8):
        loads[i].wait()

    for h in (1, 0):
        @pl.loop(0, edges // chunk, unroll=True)
        def _(i):
            rows = pl.ds(pl.multiple_of(h * edges + i * chunk, chunk), chunk)
            g = 0.5 * dot(rad[rows], wr[...])
            gate[rows] = g
            had[rows] = dot_nt(cot[rows], wb[...]) * g
            u_own[rows] = dot(p_own[rows], proj[h])

    @pl.when(relay)
    def _():
        meet()
        for c in range(COLS):
            pass_in[c].wait_recv()
            pass_on[c].start()

    for h in (1, 0):
        for c in range(COLS):
            cols = slice(c * part, (c + 1) * part)

            @pl.when(has[h])
            def _():
                halo_copies[1 - h][c].wait_recv()

            for r in range(0, edges, chunk):
                rows = slice(h * edges + r, h * edges + r + chunk)
                u = u_own[rows, cols] + dot(p_rim[rows], halo[h, c])
                p = u * gate[rows, cols]
                t = jnp.tanh(p)
                pt = p * t
                msg[rows, cols] = (p + pt).astype(BF)
                adj[rows, cols] = (had[rows, cols] * ((1.0 + t) * ((1.0 + p) - pt))).astype(BF)

            rim_out[h, c] = dot(pt_rim[h], adj[h * edges:(h + 1) * edges, cols]).astype(BF)

            @pl.when(has[h])
            def _():
                rim_copies[h][c].start()

        for r in range(0, edges, chunk):
            rows = slice(h * edges + r, h * edges + r + chunk)
            blk[rows] = dot(msg[rows], wb[...]).astype(BF)

        mine = slice(h * edges, (h + 1) * edges)
        own_part = dot(pt_own[:, mine], adj[mine])
        own_sum[...] = own_part if h == 1 else own_sum[...] + own_part
        self_adj = dot(pt_self[h], adj[mine]).astype(BF)
        fg_self[h * half:(h + 1) * half] = dot_nt(self_adj, ws[...])

    for h in (1, 0):
        rows = slice(h * half, (h + 1) * half)
        total = fg_self[rows]
        for c in range(COLS):
            cols = slice(c * part, (c + 1) * part)

            @pl.when(has[h])
            def _():
                rim_copies[1 - h][c].wait_recv()

            nbr_adj = (own_sum[rows, cols] + rim_in[h, c].astype(F32)).astype(BF)
            total = total + dot_nt(nbr_adj, wn[:, cols])
        fg[rows] = total.astype(BF)

    for side in (0, 1):
        @pl.when(has[side])
        def _():
            for copy in halo_copies[side] + rim_copies[side]:
                copy.wait_send()

    @pl.when(relay)
    def _():
        for copy in pass_on:
            copy.wait_send()


def store_kernel(blk, fg, blk_hbm, fg_hbm, sem):
    copies = [
        pltpu.make_async_copy(blk, blk_hbm, sem.at[0]),
        pltpu.make_async_copy(fg, fg_hbm, sem.at[1]),
    ]
    for copy in copies:
        copy.start()
    for copy in copies:
        copy.wait()


def body(features, radial, neighbours, counts, cotangent, w_self, w_neighbour, w_radial, w_block):
    atoms, width = features.shape
    slots = neighbours.shape[1]
    basis = radial.shape[2]
    out_width = w_block.shape[1]
    half = atoms // 2
    edges = atoms * slots
    part = width // COLS
    n_dev = lax.axis_size("cell")
    any_spec = pl.BlockSpec(memory_space=pl.ANY)
    vm = pltpu.VMEM
    dma = pltpu.SemaphoreType.DMA
    vm_spec = pl.BlockSpec(memory_space=vm)
    blocks, grad = pl.pallas_call(
        functools.partial(kernel, n_dev, slots, half, 256),
        name="edge_layer",
        out_shape=(vm((edges, out_width), BF), vm((atoms, width), BF)),
        in_specs=[any_spec] * 9,
        out_specs=(vm_spec,) * 2,
        scratch_shapes=[
            vm((atoms, width), BF), vm((edges, basis), BF), vm((slots, atoms), jnp.int32),
            vm((1, atoms), jnp.int32), vm((edges, out_width), BF), vm((width, width), BF),
            vm((width, width), BF), vm((basis, width), BF), vm((width, out_width), BF),
            vm((2, COLS, half, part), BF), vm((COLS, half, part), BF),
            vm((2, COLS, half, part), BF), vm((2, COLS, half, part), BF),
            vm((2, 3 * half, width), BF),
            vm((edges, 3 * half), BF), vm((edges, half), BF),
            vm((atoms, edges), BF), vm((2, half, edges // 2), BF), vm((2, half, edges // 2), BF),
            vm((edges, width), F32), vm((edges, width), F32), vm((edges, width), F32),
            vm((edges, width), BF), vm((edges, width), BF),
            vm((atoms, width), F32), vm((atoms, width), F32),
            dma((9,)), dma((2, COLS)), dma((2, COLS)), dma((COLS,)), dma((COLS,)),
            dma((2, COLS)), dma((2, COLS)),
        ],
        compiler_params=pltpu.CompilerParams(
            collective_id=0, has_side_effects=True, vmem_limit_bytes=56 * 1024 * 1024),
    )(
        features, radial.reshape(edges, basis), neighbours.T, counts.reshape(1, atoms),
        cotangent.reshape(edges, out_width), w_self, w_neighbour, w_radial, w_block,
    )
    blocks, grad = pl.pallas_call(
        store_kernel,
        name="store",
        out_shape=(
            jax.ShapeDtypeStruct((edges, out_width), BF),
            jax.ShapeDtypeStruct((atoms, width), BF),
        ),
        in_specs=[vm_spec] * 2,
        out_specs=(any_spec, any_spec),
        scratch_shapes=[dma((2,))],
    )(
        pltpu.with_memory_space_constraint(blocks, vm),
        pltpu.with_memory_space_constraint(grad, vm),
    )
    return blocks.reshape(atoms, slots, out_width), grad


def solution(mesh):
    in_specs = (
        P("cell", None),
        P("cell", None, None),
        P("cell", None),
        P("cell"),
        P("cell", None, None),
        P(),
        P(),
        P(),
        P(),
    )
    out_specs = (P("cell", None, None), P("cell", None))
    return jax.shard_map(body, mesh=mesh, in_specs=in_specs, out_specs=out_specs, check_vma=False)
```

time: 27.8 us -> 23.9 us (0.86)
  Pallas kernels: 27 us -> 23.1 us
    pallas_call x1, Pallas kernels: 25.9 us -> 22 us  [body(): pl.pallas_call(functools.partial(kernel, n_dev, slots, half, 256), name='...]
where the time goes in v3:
time: 23.9 us; the launch traced here: 23.8 us
  Pallas kernels  23.1 us (97%)
  between operations  0.64 us (3%)
    pallas_call x1, Pallas kernels, body(): pl.pallas_call(functools.partial(kernel, n_dev, slots, half, 256), name='...  22 us
    pallas_call x1, Pallas kernels, body(): pl.pallas_call(store_kernel, name='store', out_shape=(jax.ShapeDtypeStruc...  1.07 us

profile of v3, /device:TPU:6, one launch (start us, length us, event | category | flops | bytes accessed | tf_op | source)
XLA Modules:
  0.0 23.8 jit_solution(3059528632620915928)
XLA Ops:
  0.6 22.0 %edge_layer.1 = (bf16[2048,256]{1,0:T(8,128)(2,1)S(1)}, bf16[256,512]{1,0:T(8,128)(2,1)S(1)}) custom-call(bf16[256,512]{1,0:T(8,128)(2,1)} %feat_hbm.1, bf16[2048,128]{1,0:T(8,128)(2,1)} %bitcast.6, s32[8,256]{1,0:T(8,128)} %bitcast.7, s32[1,256]{1,0:T(1,128)} %bitcast.8, bf16[2048,256]{1,0:T(8,128)(2,1)} %bitcast.5, bf16[512,512]{1,0:T(8,128)(2,1)} %ws_hbm.1, ...), custom_call_target="tpu_custom_call" | custom-call | tf_op jit(solution)/shard_map/edge_layer/pallas_call | solution.py:286
  22.7 1.1 %store.1 = (bf16[2048,256]{1,0:T(8,128)(2,1)}, bf16[256,512]{1,0:T(8,128)(2,1)}) custom-call(bf16[2048,256]{1,0:T(8,128)(2,1)S(1)} %get-tuple-element.6.blk, bf16[256,512]{1,0:T(8,128)(2,1)S(1)} %get-tuple-element.7.fg), custom_call_target="tpu_custom_call" | custom-call | tf_op jit(solution)/shard_map/store/pallas_call | solution.py:313

commit v4 on v3

--- a/solution.py
+++ b/solution.py
@@ -11,7 +11,8 @@
 BF = jnp.bfloat16
 F32 = jnp.float32
 DEAD = 1024.0
-COLS = 2
+PARTS = ((0, 4), (4, 4))
+COLS = len(PARTS)
 ROUND = 128
 RELAY = 14
 NT = (((1,), (1,)), ((), ()))
@@ -32,10 +33,10 @@
 def kernel(
     n_dev, slots, half, chunk,
     feat_hbm, rad_hbm, nbr_hbm, cnt_hbm, cot_hbm, ws_hbm, wn_hbm, wr_hbm, wb_hbm,
-    blk, fg,
-    feat, rad, nbr, cnt, cot, ws, wn, wr, wb,
+    blk, fg_self, nbr_adj, wn,
+    feat, rad, nbr, cnt, cot, ws, wr, wb,
     halo, passed, rim_out, rim_in, proj, p_own, p_rim, pt_own, pt_rim, pt_self,
-    gate, had, u_own, msg, adj, own_sum, fg_self,
+    gate, had, u_own, msg, adj, own_sum,
     in_sem, halo_send, halo_recv, pass_send, pass_recv, rim_send, rim_recv,
 ):
     me = lax.axis_index("cell")
@@ -45,13 +46,14 @@
     far_low = jnp.logical_and(spot == ROUND - 1, has[1])
     far_high = jnp.logical_and(spot == 0, has[0])
     relay = jnp.logical_and(spot == RELAY, me + ROUND < n_dev)
+    late = jnp.logical_or(relay, me == 1)
     greet = (me - 1, jnp.where(far_low, me - (ROUND - 1 - RELAY), me + 1))
     edges = half * slots
     width = feat.shape[1]
-    part = width // COLS
+    spans = [(a * width // 8, n * width // 8) for a, n in PARTS]
 
     barrier = pltpu.get_barrier_semaphore()
-    for side in (0, 1):
+    for side in (1, 0):
         @pl.when(has[side])
         def _():
             pl.semaphore_signal(barrier, inc=1, device_id=(greet[side],), device_id_type=MESH)
@@ -67,35 +69,30 @@
     for load in loads:
         load.start()
 
-    loads[0].wait()
-    loads[1].wait()
-    own = dot(feat[...], wn[...]).astype(BF)
-    for h in (0, 1):
-        proj[h, 0:2 * half] = own
-
     halo_copies = [[
         pltpu.make_async_remote_copy(
-            src_ref=proj.at[0, pl.ds(side * half, half), pl.ds(c * part, part)],
-            dst_ref=halo.at[1 - side, c],
+            src_ref=proj.at[0, pl.ds(side * half, half), pl.ds(*spans[c])],
+            dst_ref=halo.at[1 - side, :, pl.ds(*spans[c])],
             send_sem=halo_send.at[side, c], recv_sem=halo_recv.at[1 - side, c],
             device_id=(peer[side],), device_id_type=MESH)
         for c in range(COLS)] for side in (0, 1)]
     rim_copies = [[
         pltpu.make_async_remote_copy(
-            src_ref=rim_out.at[side, c], dst_ref=rim_in.at[1 - side, c],
+            src_ref=rim_out.at[side, :, pl.ds(*spans[c])],
+            dst_ref=rim_in.at[1 - side, :, pl.ds(*spans[c])],
             send_sem=rim_send.at[side, c], recv_sem=rim_recv.at[1 - side, c],
             device_id=(peer[side],), device_id_type=MESH)
         for c in range(COLS)] for side in (0, 1)]
 
     pass_in = [
         pltpu.make_async_remote_copy(
-            src_ref=proj.at[0, pl.ds(0, half), pl.ds(c * part, part)], dst_ref=passed.at[c],
+            src_ref=proj.at[0, pl.ds(0, half), pl.ds(*spans[c])], dst_ref=passed.at[:, pl.ds(*spans[c])],
             send_sem=halo_send.at[0, c], recv_sem=pass_recv.at[c],
             device_id=(me - (ROUND - RELAY),), device_id_type=MESH)
         for c in range(COLS)]
     pass_on = [
         pltpu.make_async_remote_copy(
-            src_ref=passed.at[c], dst_ref=halo.at[1, c],
+            src_ref=passed.at[:, pl.ds(*spans[c])], dst_ref=halo.at[1, :, pl.ds(*spans[c])],
             send_sem=pass_send.at[c], recv_sem=halo_recv.at[1, c],
             device_id=(me + (ROUND - 1 - RELAY),), device_id_type=MESH)
         for c in range(COLS)]
@@ -104,6 +101,12 @@
         count = has[0].astype(jnp.int32) + has[1].astype(jnp.int32) + relay.astype(jnp.int32)
         pl.semaphore_wait(barrier, count)
 
+        @pl.when(relay)
+        def _():
+            for c in range(COLS):
+                pass_in[c].wait_recv()
+                pass_on[c].start()
+
         @pl.when(far_high)
         def _():
             for copy in pass_in:
@@ -118,16 +121,6 @@
         def _():
             for copy in halo_copies[1]:
                 copy.start()
-
-    @pl.when(jnp.logical_not(relay))
-    def _():
-        meet()
-
-    for side in (0, 1):
-        @pl.when(jnp.logical_not(has[side]))
-        def _():
-            halo[side] = jnp.zeros_like(halo[side])
-            rim_in[side] = jnp.zeros_like(rim_in[side])
 
     loads[2].wait()
     loads[3].wait()
@@ -139,7 +132,7 @@
     slot_of = slot_of % slots
     slot_sub = lax.broadcasted_iota(jnp.int32, (slots, edges), 0)
     slot_pick = slot_of == slot_sub
-    for h in (1, 0):
+    def select(h):
         ids = nbr[:, h * half:(h + 1) * half]
         shape = (slots, half)
         base = me * (2 * half) + h * half
@@ -177,14 +170,14 @@
             p_own[rows, 2 * half:3 * half] = hot(col == cs)
             p_rim[rows] = hot(col + rim_j * half == ct)
 
-    loads[4].wait()
-    for h in (0, 1):
+    def prepare(h):
+        if h == 1:
+            loads[4].wait()
         proj[h, 2 * half:3 * half] = dot(feat[h * half:(h + 1) * half], ws[...]).astype(BF)
-
-    for i in (5, 6, 7, 8):
-        loads[i].wait()
-
-    for h in (1, 0):
+        if h == 1:
+            for i in (5, 6, 7, 8):
+                loads[i].wait()
+
         @pl.loop(0, edges // chunk, unroll=True)
         def _(i):
             rows = pl.ds(pl.multiple_of(h * edges + i * chunk, chunk), chunk)
@@ -193,16 +186,9 @@
             had[rows] = dot_nt(cot[rows], wb[...]) * g
             u_own[rows] = dot(p_own[rows], proj[h])
 
-    @pl.when(relay)
-    def _():
-        meet()
+    def stages(h):
         for c in range(COLS):
-            pass_in[c].wait_recv()
-            pass_on[c].start()
-
-    for h in (1, 0):
-        for c in range(COLS):
-            cols = slice(c * part, (c + 1) * part)
+            cols = slice(spans[c][0], sum(spans[c]))
 
             @pl.when(has[h])
             def _():
@@ -210,42 +196,69 @@
 
             for r in range(0, edges, chunk):
                 rows = slice(h * edges + r, h * edges + r + chunk)
-                u = u_own[rows, cols] + dot(p_rim[rows], halo[h, c])
+                u = u_own[rows, cols] + dot(p_rim[rows], halo[h, :, cols])
                 p = u * gate[rows, cols]
                 t = jnp.tanh(p)
                 pt = p * t
                 msg[rows, cols] = (p + pt).astype(BF)
                 adj[rows, cols] = (had[rows, cols] * ((1.0 + t) * ((1.0 + p) - pt))).astype(BF)
 
-            rim_out[h, c] = dot(pt_rim[h], adj[h * edges:(h + 1) * edges, cols]).astype(BF)
+            rim_out[h, :, cols] = dot(pt_rim[h], adj[h * edges:(h + 1) * edges, cols]).astype(BF)
 
             @pl.when(has[h])
             def _():
                 rim_copies[h][c].start()
 
+    def rest(h, first):
         for r in range(0, edges, chunk):
             rows = slice(h * edges + r, h * edges + r + chunk)
             blk[rows] = dot(msg[rows], wb[...]).astype(BF)
 
         mine = slice(h * edges, (h + 1) * edges)
         own_part = dot(pt_own[:, mine], adj[mine])
-        own_sum[...] = own_part if h == 1 else own_sum[...] + own_part
+        own_sum[...] = own_part if first else own_sum[...] + own_part
         self_adj = dot(pt_self[h], adj[mine]).astype(BF)
         fg_self[h * half:(h + 1) * half] = dot_nt(self_adj, ws[...])
 
+    select(1)
+    loads[0].wait()
+    loads[1].wait()
+    own = dot(feat[...], wn[...]).astype(BF)
+    for h in (0, 1):
+        proj[h, 0:2 * half] = own
+
+    @pl.when(jnp.logical_not(late))
+    def _():
+        meet()
+
+    for side in (0, 1):
+        @pl.when(jnp.logical_not(has[side]))
+        def _():
+            halo[side] = jnp.zeros_like(halo[side])
+            rim_in[side] = jnp.zeros_like(rim_in[side])
+
+    prepare(1)
+    @pl.when(late)
+    def _():
+        meet()
+
+    stages(1)
+    select(0)
+    prepare(0)
+    stages(0)
+    rest(1, True)
+    rest(0, False)
+
     for h in (1, 0):
         rows = slice(h * half, (h + 1) * half)
-        total = fg_self[rows]
         for c in range(COLS):
-            cols = slice(c * part, (c + 1) * part)
+            cols = slice(spans[c][0], sum(spans[c]))
 
             @pl.when(has[h])
             def _():
                 rim_copies[1 - h][c].wait_recv()
 
-            nbr_adj = (own_sum[rows, cols] + rim_in[h, c].astype(F32)).astype(BF)
-            total = total + dot_nt(nbr_adj, wn[:, cols])
-        fg[rows] = total.astype(BF)
+            nbr_adj[rows, cols] = (own_sum[rows, cols] + rim_in[h, :, cols].astype(F32)).astype(BF)
 
     for side in (0, 1):
         @pl.when(has[side])
@@ -259,13 +272,15 @@
             copy.wait_send()
 
 
-def store_kernel(blk, fg, blk_hbm, fg_hbm, sem):
-    copies = [
-        pltpu.make_async_copy(blk, blk_hbm, sem.at[0]),
-        pltpu.make_async_copy(fg, fg_hbm, sem.at[1]),
-    ]
-    for copy in copies:
-        copy.start()
+def finish_kernel(blk, fg_self, nbr_adj, wn, blk_hbm, fg_hbm, fg, sem):
+    copies = [pltpu.make_async_copy(blk, blk_hbm, sem.at[2])]
+    copies[0].start()
+    half = fg.shape[0] // 2
+    for h in (0, 1):
+        rows = pl.ds(h * half, half)
+        fg[rows] = (fg_self[rows] + dot_nt(nbr_adj[rows], wn[...])).astype(BF)
+        copies.append(pltpu.make_async_copy(fg.at[rows], fg_hbm.at[rows], sem.at[h]))
+        copies[-1].start()
     for copy in copies:
         copy.wait()
 
@@ -277,30 +292,32 @@
     out_width = w_block.shape[1]
     half = atoms // 2
     edges = atoms * slots
-    part = width // COLS
     n_dev = lax.axis_size("cell")
     any_spec = pl.BlockSpec(memory_space=pl.ANY)
     vm = pltpu.VMEM
     dma = pltpu.SemaphoreType.DMA
     vm_spec = pl.BlockSpec(memory_space=vm)
-    blocks, grad = pl.pallas_call(
+    parts = pl.pallas_call(
         functools.partial(kernel, n_dev, slots, half, 256),
         name="edge_layer",
-        out_shape=(vm((edges, out_width), BF), vm((atoms, width), BF)),
+        out_shape=(
+            vm((edges, out_width), BF), vm((atoms, width), F32),
+            vm((atoms, width), BF), vm((width, width), BF),
+        ),
         in_specs=[any_spec] * 9,
-        out_specs=(vm_spec,) * 2,
+        out_specs=(vm_spec,) * 4,
         scratch_shapes=[
             vm((atoms, width), BF), vm((edges, basis), BF), vm((slots, atoms), jnp.int32),
             vm((1, atoms), jnp.int32), vm((edges, out_width), BF), vm((width, width), BF),
-            vm((width, width), BF), vm((basis, width), BF), vm((width, out_width), BF),
-            vm((2, COLS, half, part), BF), vm((COLS, half, part), BF),
-            vm((2, COLS, half, part), BF), vm((2, COLS, half, part), BF),
+            vm((basis, width), BF), vm((width, out_width), BF),
+            vm((2, half, width), BF), vm((half, width), BF),
+            vm((2, half, width), BF), vm((2, half, width), BF),
             vm((2, 3 * half, width), BF),
             vm((edges, 3 * half), BF), vm((edges, half), BF),
             vm((atoms, edges), BF), vm((2, half, edges // 2), BF), vm((2, half, edges // 2), BF),
             vm((edges, width), F32), vm((edges, width), F32), vm((edges, width), F32),
             vm((edges, width), BF), vm((edges, width), BF),
-            vm((atoms, width), F32), vm((atoms, width), F32),
+            vm((atoms, width), F32),
             dma((9,)), dma((2, COLS)), dma((2, COLS)), dma((COLS,)), dma((COLS,)),
             dma((2, COLS)), dma((2, COLS)),
         ],
@@ -311,19 +328,16 @@
         cotangent.reshape(edges, out_width), w_self, w_neighbour, w_radial, w_block,
     )
     blocks, grad = pl.pallas_call(
-        store_kernel,
-        name="store",
+        finish_kernel,
+        name="finish",
         out_shape=(
             jax.ShapeDtypeStruct((edges, out_width), BF),
             jax.ShapeDtypeStruct((atoms, width), BF),
         ),
-        in_specs=[vm_spec] * 2,
+        in_specs=[vm_spec] * 4,
         out_specs=(any_spec, any_spec),
-        scratch_shapes=[dma((2,))],
-    )(
-        pltpu.with_memory_space_constraint(blocks, vm),
-        pltpu.with_memory_space_constraint(grad, vm),
-    )
+        scratch_shapes=[vm((atoms, width), BF), dma((3,))],
+    )(*[pltpu.with_memory_space_constraint(array, vm) for array in parts])
     return blocks.reshape(atoms, slots, out_width), grad
 
 

time: 23.9 us -> 22.9 us (0.958)
  Pallas kernels: 23.1 us -> 22.1 us
    pallas_call x1, Pallas kernels: 22 us -> 20.9 us  [body(): pl.pallas_call(functools.partial(kernel, n_dev, slots, half, 256), name='...]
where the time goes in v4:
time: 22.9 us; the launch traced here: 22.7 us
  Pallas kernels  22.1 us (97%)
  between operations  0.64 us (3%)
    pallas_call x1, Pallas kernels, body(): pl.pallas_call(functools.partial(kernel, n_dev, slots, half, 256), name='...  20.9 us
    pallas_call x1, Pallas kernels, body(): pl.pallas_call(finish_kernel, name='finish', out_shape=(jax.ShapeDtypeStr...  1.16 us

profile of v4, /device:TPU:6, one launch (start us, length us, event | category | flops | bytes accessed | tf_op | source)
XLA Modules:
  0.0 22.7 jit_solution(2746413279019579097)
XLA Ops:
  0.6 20.9 %edge_layer.1 = (bf16[2048,256]{1,0:T(8,128)(2,1)S(1)}, f32[256,512]{1,0:T(8,128)S(1)}, bf16[256,512]{1,0:T(8,128)(2,1)S(1)}, bf16[512,512]{1,0:T(8,128)(2,1)S(1)}) custom-call(bf16[256,512]{1,0:T(8,128)(2,1)} %feat_hbm.1, bf16[2048,128]{1,0:T(8,128)(2,1)} %bitcast.6, s32[8,256]{1,0:T(8,128)} %bitcast.7, s32[1,256]{1,0:T(1,128)} %bitcast.8, ...), custom_call_target="tpu_custom_call" | custom-call | tf_op jit(solution)/shard_map/edge_layer/pallas_call | solution.py:300
  21.6 1.2 %finish.1 = (bf16[2048,256]{1,0:T(8,128)(2,1)}, bf16[256,512]{1,0:T(8,128)(2,1)}) custom-call(bf16[2048,256]{1,0:T(8,128)(2,1)S(1)} %get-tuple-element.8.blk, f32[256,512]{1,0:T(8,128)S(1)} %get-tuple-element.9.fg_self, bf16[256,512]{1,0:T(8,128)(2,1)S(1)} %get-tuple-element.10.nbr_adj, bf16[512,512]{1,0:T(8,128)(2,1)S(1)} %get-tuple-element.11.wn), custom_call_target="tpu_custom_call" | custom-call | tf_op jit(solution)/shard_map/finish/pallas_call | solution.py:330

commit v5 on v4

--- a/solution.py
+++ b/solution.py
@@ -33,10 +33,10 @@
 def kernel(
     n_dev, slots, half, chunk,
     feat_hbm, rad_hbm, nbr_hbm, cnt_hbm, cot_hbm, ws_hbm, wn_hbm, wr_hbm, wb_hbm,
-    blk, fg_self, nbr_adj, wn,
+    blk, fg_high, fg_low, nbr_adj, wn,
     feat, rad, nbr, cnt, cot, ws, wr, wb,
     halo, passed, rim_out, rim_in, proj, p_own, p_rim, pt_own, pt_rim, pt_self,
-    gate, had, u_own, msg, adj, own_sum,
+    gate, had, u_own, msg, adj, own_sum, fg_part,
     in_sem, halo_send, halo_recv, pass_send, pass_recv, rim_send, rim_recv,
 ):
     me = lax.axis_index("cell")
@@ -194,16 +194,19 @@
             def _():
                 halo_copies[1 - h][c].wait_recv()
 
-            for r in range(0, edges, chunk):
-                rows = slice(h * edges + r, h * edges + r + chunk)
+            rim = None
+            for r in range(0, edges, 128):
+                rows = slice(h * edges + r, h * edges + r + 128)
                 u = u_own[rows, cols] + dot(p_rim[rows], halo[h, :, cols])
                 p = u * gate[rows, cols]
                 t = jnp.tanh(p)
                 pt = p * t
                 msg[rows, cols] = (p + pt).astype(BF)
-                adj[rows, cols] = (had[rows, cols] * ((1.0 + t) * ((1.0 + p) - pt))).astype(BF)
-
-            rim_out[h, :, cols] = dot(pt_rim[h], adj[h * edges:(h + 1) * edges, cols]).astype(BF)
+                adjoint = (had[rows, cols] * ((1.0 + t) * ((1.0 + p) - pt))).astype(BF)
+                adj[rows, cols] = adjoint
+                piece = dot(pt_rim[h, :, r:r + 128], adjoint)
+                rim = piece if rim is None else rim + piece
+            rim_out[h, :, cols] = rim.astype(BF)
 
             @pl.when(has[h])
             def _():
@@ -218,7 +221,8 @@
         own_part = dot(pt_own[:, mine], adj[mine])
         own_sum[...] = own_part if first else own_sum[...] + own_part
         self_adj = dot(pt_self[h], adj[mine]).astype(BF)
-        fg_self[h * half:(h + 1) * half] = dot_nt(self_adj, ws[...])
+        fg_self = fg_part if h == 1 else fg_low
+        fg_self[...] = dot_nt(self_adj, ws[...])
 
     select(1)
     loads[0].wait()
@@ -258,7 +262,13 @@
             def _():
                 rim_copies[1 - h][c].wait_recv()
 
-            nbr_adj[rows, cols] = (own_sum[rows, cols] + rim_in[h, :, cols].astype(F32)).astype(BF)
+            total = (own_sum[rows, cols] + rim_in[h, :, cols].astype(F32)).astype(BF)
+            if h == 1:
+                fg_part[...] += dot_nt(total, wn[:, cols])
+            else:
+                nbr_adj[:, cols] = total
+        if h == 1:
+            fg_high[...] = fg_part[...].astype(BF)
 
     for side in (0, 1):
         @pl.when(has[side])
@@ -272,15 +282,17 @@
             copy.wait_send()
 
 
-def finish_kernel(blk, fg_self, nbr_adj, wn, blk_hbm, fg_hbm, fg, sem):
-    copies = [pltpu.make_async_copy(blk, blk_hbm, sem.at[2])]
+def finish_kernel(blk, fg_high, fg_low, nbr_adj, wn, blk_hbm, fg_hbm, fg, sem):
+    half = fg.shape[0]
+    copies = [
+        pltpu.make_async_copy(blk, blk_hbm, sem.at[0]),
+        pltpu.make_async_copy(fg_high, fg_hbm.at[pl.ds(half, half)], sem.at[1]),
+        pltpu.make_async_copy(fg, fg_hbm.at[pl.ds(0, half)], sem.at[2]),
+    ]
     copies[0].start()
-    half = fg.shape[0] // 2
-    for h in (0, 1):
-        rows = pl.ds(h * half, half)
-        fg[rows] = (fg_self[rows] + dot_nt(nbr_adj[rows], wn[...])).astype(BF)
-        copies.append(pltpu.make_async_copy(fg.at[rows], fg_hbm.at[rows], sem.at[h]))
-        copies[-1].start()
+    copies[1].start()
+    fg[...] = (fg_low[...] + dot_nt(nbr_adj[...], wn[...])).astype(BF)
+    copies[2].start()
     for copy in copies:
         copy.wait()
 
@@ -301,11 +313,11 @@
         functools.partial(kernel, n_dev, slots, half, 256),
         name="edge_layer",
         out_shape=(
-            vm((edges, out_width), BF), vm((atoms, width), F32),
-            vm((atoms, width), BF), vm((width, width), BF),
+            vm((edges, out_width), BF), vm((half, width), BF), vm((half, width), F32),
+            vm((half, width), BF), vm((width, width), BF),
         ),
         in_specs=[any_spec] * 9,
-        out_specs=(vm_spec,) * 4,
+        out_specs=(vm_spec,) * 5,
         scratch_shapes=[
             vm((atoms, width), BF), vm((edges, basis), BF), vm((slots, atoms), jnp.int32),
             vm((1, atoms), jnp.int32), vm((edges, out_width), BF), vm((width, width), BF),
@@ -317,7 +329,7 @@
             vm((atoms, edges), BF), vm((2, half, edges // 2), BF), vm((2, half, edges // 2), BF),
             vm((edges, width), F32), vm((edges, width), F32), vm((edges, width), F32),
             vm((edges, width), BF), vm((edges, width), BF),
-            vm((atoms, width), F32),
+            vm((atoms, width), F32), vm((half, width), F32),
             dma((9,)), dma((2, COLS)), dma((2, COLS)), dma((COLS,)), dma((COLS,)),
             dma((2, COLS)), dma((2, COLS)),
         ],
@@ -334,9 +346,9 @@
             jax.ShapeDtypeStruct((edges, out_width), BF),
             jax.ShapeDtypeStruct((atoms, width), BF),
         ),
-        in_specs=[vm_spec] * 4,
+        in_specs=[vm_spec] * 5,
         out_specs=(any_spec, any_spec),
-        scratch_shapes=[vm((atoms, width), BF), dma((3,))],
+        scratch_shapes=[vm((half, width), BF), dma((3,))],
     )(*[pltpu.with_memory_space_constraint(array, vm) for array in parts])
     return blocks.reshape(atoms, slots, out_width), grad
 

time: 22.9 us -> 22.8 us (level)
  no operation moved by 1% of the time
where the time goes in v5:
time: 22.8 us; the launch traced here: 22.7 us
  Pallas kernels  22.1 us (97%)
  between operations  0.64 us (3%)
    pallas_call x1, Pallas kernels, body(): pl.pallas_call(functools.partial(kernel, n_dev, slots, half, 256), name='...  20.9 us
    pallas_call x1, Pallas kernels, body(): pl.pallas_call(finish_kernel, name='finish', out_shape=(jax.ShapeDtypeStr...  1.15 us

profile of v5, /device:TPU:6, one launch (start us, length us, event | category | flops | bytes accessed | tf_op | source)
XLA Modules:
  0.0 22.7 jit_solution(14698620090745465767)
XLA Ops:
  0.6 20.9 %edge_layer.1 = (bf16[2048,256]{1,0:T(8,128)(2,1)S(1)}, bf16[128,512]{1,0:T(8,128)(2,1)S(1)}, f32[128,512]{1,0:T(8,128)S(1)}, bf16[128,512]{1,0:T(8,128)(2,1)S(1)}, bf16[512,512]{1,0:T(8,128)(2,1)S(1)}) custom-call(bf16[256,512]{1,0:T(8,128)(2,1)} %feat_hbm.1, bf16[2048,128]{1,0:T(8,128)(2,1)} %bitcast.6, s32[8,256]{1,0:T(8,128)} %bitcast.7, ...), custom_call_target="tpu_custom_call" | custom-call | tf_op jit(solution)/shard_map/edge_layer/pallas_call | solution.py:312
  21.6 1.1 %finish.1 = (bf16[2048,256]{1,0:T(8,128)(2,1)}, bf16[256,512]{1,0:T(8,128)(2,1)}) custom-call(bf16[2048,256]{1,0:T(8,128)(2,1)S(1)} %get-tuple-element.9.blk, bf16[128,512]{1,0:T(8,128)(2,1)S(1)} %get-tuple-element.10.fg_high, f32[128,512]{1,0:T(8,128)S(1)} %get-tuple-element.11.fg_low, bf16[128,512]{1,0:T(8,128)(2,1)S(1)} %get-tuple-element.12.nbr_adj, ...), custom_call_target="tpu_custom_call" | custom-call | tf_op jit(solution)/shard_map/finish/pallas_call | solution.py:342

commit v6 on v5

--- a/solution.py
+++ b/solution.py
@@ -14,7 +14,7 @@
 PARTS = ((0, 4), (4, 4))
 COLS = len(PARTS)
 ROUND = 128
-RELAY = 14
+RELAY = 15
 NT = (((1,), (1,)), ((), ()))
 
 
@@ -247,10 +247,10 @@
         meet()
 
     stages(1)
+    rest(1, True)
     select(0)
     prepare(0)
     stages(0)
-    rest(1, True)
     rest(0, False)
 
     for h in (1, 0):

time: 22.8 us -> 22.3 us (0.978)
  Pallas kernels: 22.1 us -> 21.5 us
    pallas_call x1, Pallas kernels: 20.9 us -> 20.3 us  [body(): pl.pallas_call(functools.partial(kernel, n_dev, slots, half, 256), name='...]
where the time goes in v6:
time: 22.3 us; the launch traced here: 22.1 us
  Pallas kernels  21.5 us (96%)
  between operations  0.64 us (3%)
    pallas_call x1, Pallas kernels, body(): pl.pallas_call(functools.partial(kernel, n_dev, slots, half, 256), name='...  20.3 us
    pallas_call x1, Pallas kernels, body(): pl.pallas_call(finish_kernel, name='finish', out_shape=(jax.ShapeDtypeStr...  1.15 us

profile of v6, /device:TPU:6, one launch (start us, length us, event | category | flops | bytes accessed | tf_op | source)
XLA Modules:
  0.0 22.1 jit_solution(8545254529246545534)
XLA Ops:
  0.6 20.3 %edge_layer.1 = (bf16[2048,256]{1,0:T(8,128)(2,1)S(1)}, bf16[128,512]{1,0:T(8,128)(2,1)S(1)}, f32[128,512]{1,0:T(8,128)S(1)}, bf16[128,512]{1,0:T(8,128)(2,1)S(1)}, bf16[512,512]{1,0:T(8,128)(2,1)S(1)}) custom-call(bf16[256,512]{1,0:T(8,128)(2,1)} %feat_hbm.1, bf16[2048,128]{1,0:T(8,128)(2,1)} %bitcast.6, s32[8,256]{1,0:T(8,128)} %bitcast.7, ...), custom_call_target="tpu_custom_call" | custom-call | tf_op jit(solution)/shard_map/edge_layer/pallas_call | solution.py:312
  21.0 1.1 %finish.1 = (bf16[2048,256]{1,0:T(8,128)(2,1)}, bf16[256,512]{1,0:T(8,128)(2,1)}) custom-call(bf16[2048,256]{1,0:T(8,128)(2,1)S(1)} %get-tuple-element.9.blk, bf16[128,512]{1,0:T(8,128)(2,1)S(1)} %get-tuple-element.10.fg_high, f32[128,512]{1,0:T(8,128)S(1)} %get-tuple-element.11.fg_low, bf16[128,512]{1,0:T(8,128)(2,1)S(1)} %get-tuple-element.12.nbr_adj, ...), custom_call_target="tpu_custom_call" | custom-call | tf_op jit(solution)/shard_map/finish/pallas_call | solution.py:342

commit v7 on v6

--- a/solution.py
+++ b/solution.py
@@ -107,6 +107,11 @@
                 pass_in[c].wait_recv()
                 pass_on[c].start()
 
+        @pl.when(has[1])
+        def _():
+            for copy in halo_copies[1]:
+                copy.start()
+
         @pl.when(far_high)
         def _():
             for copy in pass_in:
@@ -115,11 +120,6 @@
         @pl.when(jnp.logical_and(has[0], jnp.logical_not(far_high)))
         def _():
             for copy in halo_copies[0]:
-                copy.start()
-
-        @pl.when(has[1])
-        def _():
-            for copy in halo_copies[1]:
                 copy.start()
 
     loads[2].wait()

time: 22.3 us -> 22.3 us (level)
  no operation moved by 1% of the time
where the time goes in v7:
time: 22.3 us; the launch traced here: 22.1 us
  Pallas kernels  21.5 us (96%)
  between operations  0.64 us (3%)
    pallas_call x1, Pallas kernels, body(): pl.pallas_call(functools.partial(kernel, n_dev, slots, half, 256), name='...  20.3 us
    pallas_call x1, Pallas kernels, body(): pl.pallas_call(finish_kernel, name='finish', out_shape=(jax.ShapeDtypeStr...  1.15 us

profile of v7, /device:TPU:6, one launch (start us, length us, event | category | flops | bytes accessed | tf_op | source)
XLA Modules:
  0.0 22.1 jit_solution(5571214317664115648)
XLA Ops:
  0.6 20.3 %edge_layer.1 = (bf16[2048,256]{1,0:T(8,128)(2,1)S(1)}, bf16[128,512]{1,0:T(8,128)(2,1)S(1)}, f32[128,512]{1,0:T(8,128)S(1)}, bf16[128,512]{1,0:T(8,128)(2,1)S(1)}, bf16[512,512]{1,0:T(8,128)(2,1)S(1)}) custom-call(bf16[256,512]{1,0:T(8,128)(2,1)} %feat_hbm.1, bf16[2048,128]{1,0:T(8,128)(2,1)} %bitcast.6, s32[8,256]{1,0:T(8,128)} %bitcast.7, ...), custom_call_target="tpu_custom_call" | custom-call | tf_op jit(solution)/shard_map/edge_layer/pallas_call | solution.py:312
  21.0 1.1 %finish.1 = (bf16[2048,256]{1,0:T(8,128)(2,1)}, bf16[256,512]{1,0:T(8,128)(2,1)}) custom-call(bf16[2048,256]{1,0:T(8,128)(2,1)S(1)} %get-tuple-element.9.blk, bf16[128,512]{1,0:T(8,128)(2,1)S(1)} %get-tuple-element.10.fg_high, f32[128,512]{1,0:T(8,128)S(1)} %get-tuple-element.11.fg_low, bf16[128,512]{1,0:T(8,128)(2,1)S(1)} %get-tuple-element.12.nbr_adj, ...), custom_call_target="tpu_custom_call" | custom-call | tf_op jit(solution)/shard_map/finish/pallas_call | solution.py:342
